TPU v7x, 256 devices: a whole 4x4x8 slice. The times are simulated.
256 devices in a mesh: cuts: 16 (over y, x_lo, core), pencil: 16 (over z, x_hi).
Axes of the slice: x: 4 (x_hi: 2, x_lo: 2; x = x_hi * 2 + x_lo), y: 4, z: 8, core: 2. Of those that a mesh axis runs over, the one named last changes fastest.
Arguments:
- wavefunctions: bfloat16 [64, 9216, 192], P('cuts', 'pencil'), may hold values from -8 to 8
- potential: float32 [192, 192, 192], P('pencil'), may hold values from -6 to 6
- keep_mask: int32 [16, 2, 2], P('cuts'), may hold values 0 or 1
- stick_map: int32 [9216], P('pencil'), may hold values from 0 to 575, as said below
Outputs:
- hamiltonian_bands: bfloat16 [64, 9216, 192], P('cuts', 'pencil')
Inputs may be any that keep to these rules, and one draw needn't show every extreme that they name: `stick_map`: each block of 576 consecutive entries (one index of pencil) is a permutation of 0 to 575.
All inputs are finite; a program needn't handle non-finite values. No bound on the sum of `keep_mask` on one device may be relied on, other than what follows from the above.
Results may differ from a plain program's by a relative error of at most 0.0065.
Values may be sent and summed in bfloat16 or wider, within the bound.
No kernel may reach another device: no remote copies, remote signals or barrier semaphores. Data moves between devices by JAX's collectives and lax.ppermute only.
A program may use at most 128 MiB of HBM per device.

v0:
```python
import math

import jax
import jax.numpy as jnp
from jax import lax
from jax.sharding import PartitionSpec as P

GRID = 192
EDGE = 2
GBOX = 96


def from_behind(block, axis, distance):
    devices = range(lax.axis_size(axis))
    route = [(i - distance, i) for i in devices if i - distance in devices]
    return lax.ppermute(block, axis, route)


def dft_tables(box_size, length):
    frequency = jnp.arange(box_size, dtype=jnp.float32) - float(box_size // 2)
    points = jnp.arange(length, dtype=jnp.float32)
    phases = 2.0 * math.pi / length * jnp.mod(frequency[:, None] * points[None, :], float(length))
    ahead_scale = 1.0 / math.sqrt(box_size)
    behind_scale = math.sqrt(box_size) / length
    ahead_cos = (jnp.cos(phases) * ahead_scale).astype(jnp.bfloat16)
    ahead_sin = (jnp.sin(phases) * ahead_scale).astype(jnp.bfloat16)
    behind_cos = (jnp.cos(phases).T * behind_scale).astype(jnp.bfloat16)
    behind_sin = (-jnp.sin(phases).T * behind_scale).astype(jnp.bfloat16)
    return (ahead_cos, ahead_sin, behind_cos, behind_sin)


def last_matrix(cos_table, sin_table):
    upper_rows = jnp.concatenate([cos_table, sin_table], axis=1)
    lower_rows = jnp.concatenate([-sin_table, cos_table], axis=1)
    return jnp.concatenate([upper_rows, lower_rows], axis=0)


def combine_halves(cos_part, sin_part):
    middle = cos_part.shape[-1] // 2
    real_part = cos_part[..., :middle] - sin_part[..., middle:]
    imag_part = sin_part[..., :middle] + cos_part[..., middle:]
    return jnp.concatenate([real_part, imag_part], axis=-1)


def along_axis(values, cos_table, sin_table, pattern):
    cos_part = jnp.einsum(pattern, values, cos_table, preferred_element_type=jnp.float32)
    sin_part = jnp.einsum(pattern, values, sin_table, preferred_element_type=jnp.float32)
    return combine_halves(cos_part, sin_part)


def along_last(values, matrix):
    return jnp.einsum("bxyc,cd->bxyd", values, matrix, preferred_element_type=jnp.float32)


def kinetic_table(box_size, row_start, column_count):
    center = box_size // 2
    freq_rows = jnp.arange(box_size, dtype=jnp.float32) - center
    freq_cols = (row_start + jnp.arange(column_count, dtype=jnp.int32)).astype(jnp.float32) - center
    freq_depth = jnp.arange(box_size, dtype=jnp.float32) - center
    freq_depth = jnp.concatenate([freq_depth, freq_depth])
    squares = (
        freq_rows[:, None, None] ** 2
        + freq_cols[None, :, None] ** 2
        + freq_depth[None, None, :] ** 2
    )
    return 0.5 * squares / float(center * center)


def local(wavefunctions, potential, keep_mask, stick_map):
    bands_dev, sticks_dev, row_width = wavefunctions.shape
    middle = row_width // 2
    rows_local = sticks_dev // GBOX
    precise = lax.Precision.HIGHEST
    upper_edge = wavefunctions[bands_dev - EDGE :]
    lower_edge = wavefunctions[:EDGE].astype(jnp.float32)
    neighbor = from_behind(upper_edge, "cuts", 1).astype(jnp.float32)
    correlation_real = jnp.einsum("jgc,igc->ji", neighbor, lower_edge, precision=precise)
    correlation_imag = jnp.einsum(
        "jgc,igc->ji", neighbor[..., :middle], lower_edge[..., middle:], precision=precise
    ) - jnp.einsum(
        "jgc,igc->ji", neighbor[..., middle:], lower_edge[..., :middle], precision=precise
    )
    neighbor_norms = jnp.sum(neighbor * neighbor, axis=(1, 2))
    correlation_real, correlation_imag, neighbor_norms = lax.psum(
        (correlation_real, correlation_imag, neighbor_norms), "pencil"
    )
    divisor = neighbor_norms[None, :] + 1e-05
    keep_factor = keep_mask[0].astype(jnp.float32)
    weight_real = keep_factor * correlation_real.T / divisor
    weight_imag = keep_factor * correlation_imag.T / divisor
    cos_part = jnp.einsum("ij,jgc->igc", weight_real, neighbor, precision=precise)
    sin_part = jnp.einsum("ij,jgc->igc", weight_imag, neighbor, precision=precise)
    new_lower = (lower_edge - combine_halves(cos_part, sin_part)).astype(jnp.bfloat16)
    ortho = jnp.concatenate([new_lower, wavefunctions[EDGE:]], axis=0)
    inverse = (
        jnp.zeros((sticks_dev,), jnp.int32)
        .at[stick_map]
        .set(jnp.arange(sticks_dev, dtype=jnp.int32))
    )
    freq_block = jnp.take(ortho, inverse, axis=1).reshape(bands_dev, GBOX, rows_local, row_width)
    ahead_cos, ahead_sin, behind_cos, behind_sin = dft_tables(GBOX, GRID)
    ahead_last = last_matrix(ahead_cos, ahead_sin)
    behind_last = last_matrix(behind_cos, behind_sin)
    doubled = jnp.concatenate([potential, potential], axis=-1)
    section_one = along_axis(freq_block, ahead_cos, ahead_sin, "bkyc,kn->bnyc").astype(jnp.bfloat16)
    section_two = along_last(section_one, ahead_last).astype(jnp.bfloat16)
    real_space = along_axis(
        lax.all_to_all(section_two, "pencil", split_axis=1, concat_axis=2, tiled=True),
        ahead_cos,
        ahead_sin,
        "bxkc,kn->bxnc",
    ).astype(jnp.bfloat16)
    scaled = (doubled * real_space.astype(jnp.float32)).astype(jnp.bfloat16)
    back_one = along_axis(scaled, behind_cos, behind_sin, "bxnc,nk->bxkc").astype(jnp.bfloat16)
    back_one = lax.all_to_all(back_one, "pencil", split_axis=2, concat_axis=1, tiled=True)
    back_two = along_last(back_one, behind_last).astype(jnp.bfloat16)
    back_three = along_axis(back_two, behind_cos, behind_sin, "bnyc,nk->bkyc")
    row_start = lax.axis_index("pencil") * rows_local
    kinetic = kinetic_table(GBOX, row_start, rows_local)
    result = (back_three + kinetic * freq_block.astype(jnp.float32)).astype(jnp.bfloat16)
    result = result.reshape(bands_dev, sticks_dev, row_width)
    return jnp.take(result, stick_map, axis=1)


def solution(mesh):
    return jax.shard_map(
        local,
        mesh=mesh,
        in_specs=(
            P("cuts", "pencil", None),
            P("pencil", None, None),
            P("cuts", None, None),
            P("pencil"),
        ),
        out_specs=P("cuts", "pencil", None),
        check_vma=False,
    )
```

profile of v0, /device:TPU:10, one launch (start us, length us, event | category | flops | bytes accessed | tf_op | source)
XLA Modules:
  0.0 317.6 jit_solution(9115159677864080000)
XLA Ops:
  1.8 1.9 collective-permute-start
  5.4 4.1 %scatter_custom_fusion = s32[576]{0:T(1024)S(1)} fusion(s32[576]{0:T(1024)S(1)} %compare_select_fusion, s32[576]{0:T(1024)S(1)} %iota.60, s32[]{:T(128)} %constant.27.clone.1), kind=kCustom, calls=%fused_computation.101 | custom fusion | bytes 2308 | tf_op jit(solution)/shard_map/scatter | solution.py:98
  13.7 1.4 convolution_bitcast_fusion.6
  15.7 44.3 %all-reduce = (f32[2,2]{1,0:T(2,128)S(1)}, f32[2]{0:T(128)S(1)}, f32[2,2]{1,0:T(2,128)S(1)}) all-reduce(f32[2,2]{1,0:T(2,128)S(1)} %convolution_bitcast_fusion.6, f32[2]{0:T(128)S(1)} %multiply_reduce_fusion, f32[2,2]{1,0:T(2,128)S(1)} %fusion.18), channel_id=1, replica_groups=mesh['cuts'=16,'pencil'=16] {'pencil'}, use_global_device_ids=true, to_apply=%region_0.0 | all-reduce | flops 10 | bytes 80 | tf_op jit(solution)/shard_map/psum | solution.py:84
  60.0 1.7 fusion.59
  61.7 1.7 fusion.61
  65.7 1.9 copy.65
  67.6 3.2 %gather_fusion = bf16[576,4,192]{2,1,0:T(4,128)(2,1)S(1)} fusion(bf16[4,576,192]{2,0,1:T(4,128)(2,1)S(1)} %copy.65, s32[1024]{0:T(1024)S(1)} %pad_clamp_fusion.1), kind=kCustom, calls=%fused_computation.clone | custom fusion | bytes 1771776 | tf_op jit(solution)/shard_map/jit(_take)/gather | solution.py:100
  70.9 2.1 broadcast_select_fusion
  73.0 1.7 copy.66
  77.2 1.3 fusion.9
  78.5 1.5 convolution_convert_fusion
  80.0 4.5 %copy.69 = bf16[4,192,6,384]{3,0,2,1:T(4,128)(2,1)} copy(bf16[4,192,6,384]{3,1,2,0:T(8,128)(2,1)S(1)} %convolution_convert_fusion) | data formatting | bytes 7077888 | tf_op jit(solution)/shard_map/convert_element_type | solution.py:106
  84.5 4.3 %all-to-all-start = ((bf16[4,192,6,384]{3,0,2,1:T(4,128)(2,1)}), bf16[4,192,6,384]{3,0,2,1:T(4,128)(2,1)S(1)}, u32[]{:S(2)}, u32[]{:S(2)}) async-start(bf16[4,192,6,384]{3,0,2,1:T(4,128)(2,1)} %copy.69), calls=%async_computation | async-start | bytes 7077888 | tf_op jit(solution)/shard_map/all_to_all | solution.py:108
  88.8 4.9 %pad_maximum_fusion = f32[12,192,384]{2,1,0:T(8,128)} fusion(f32[12,192,192]{2,1,0:T(8,128)} %param.7), kind=kLoop, calls=%fused_computation.14 | loop fusion | flops 884736 | bytes 5308416 | tf_op jit(solution)/shard_map/concatenate | solution.py:104
  93.7 71.0 %all-to-all-done = bf16[4,192,6,384]{3,0,2,1:T(4,128)(2,1)S(1)} async-done(((bf16[4,192,6,384]{3,0,2,1:T(4,128)(2,1)}), bf16[4,192,6,384]{3,0,2,1:T(4,128)(2,1)S(1)}, u32[]{:S(2)}, u32[]{:S(2)}) %all-to-all-start) | async-done | bytes 3538976 | tf_op jit(solution)/shard_map/all_to_all | solution.py:108
  164.7 1.5 copy.70
  166.3 2.5 convolution_bitcast_fusion.1
  168.7 7.5 %convolution_bitcast_fusion = f32[4,12,192,384]{3,2,1,0:T(8,128)} fusion(bf16[4,12,96,384]{3,0,2,1:T(4,128)(2,1)S(1)} %bitcast.112, f32[96]{0:T(128)S(1)} %iota_add_fusion), kind=kOutput, calls=%fused_computation.8 | convolution fusion | flops 679661568 | bytes 17695104 | tf_op jit(solution)/shard_map/bxkc,kn->bxnc/dot_general | solution.py:47
  176.3 11.9 %fusion.1 = (bf16[4,12,192,192]{3,2,1,0:T(8,128)(2,1)S(1)}, bf16[4,12,192,192]{3,2,1,0:T(8,128)(2,1)}) fusion(f32[4,12,192,384]{3,2,1,0:T(8,128)} %convolution_bitcast_fusion, f32[4,12,192,384]{3,2,1,0:T(8,128)S(1)} %convolution_bitcast_fusion.1), kind=kLoop, calls=%fused_computation.7 | loop fusion | flops 7077888 | bytes 35389440 | tf_op jit(solution)/shard_map/convert.2
  188.2 6.8 %convolution_bitcast_fusion.3 = f32[4,12,96,384]{3,2,1,0:T(8,128)S(1)} fusion(bf16[4,12,192,192]{3,2,1,0:T(8,128)(2,1)} %get-tuple-element.10, bf16[4,12,192,192]{3,2,1,0:T(8,128)(2,1)S(1)} %get-tuple-element.9, f32[12,192,384]{2,1,0:T(8,128)} %pad_maximum_fusion, f32[96]{0:T(128)S(1)} %iota_add_fusion), kind=kOutput, calls=%fused_computation.21 | convolution fusion | flops 700895232 | bytes 17695104 | tf_op jit(solution)/shard_map/bxnc,nk->bxkc/dot_general | solution.py:46
  195.0 6.3 %convolution_bitcast_fusion.2 = f32[4,12,96,384]{3,2,1,0:T(8,128)} fusion(bf16[4,12,192,192]{3,2,1,0:T(8,128)(2,1)S(1)} %copy-done, bf16[4,12,192,192]{3,2,1,0:T(8,128)(2,1)S(1)} %get-tuple-element.9, f32[12,192,384]{2,1,0:T(8,128)S(1)} %copy-done.1, f32[96]{0:T(128)S(1)} %iota_add_fusion), kind=kOutput, calls=%fused_computation.20 | convolution fusion | flops 700913664 | bytes 17695104 | tf_op jit(solution)/shard_map/bxnc,nk->bxkc/dot_general | solution.py:47
  201.3 5.4 %fusion.3 = (bf16[4,12,96,192]{3,2,1,0:T(8,128)(2,1)S(1)}, bf16[4,12,96,192]{3,2,1,0:T(8,128)(2,1)S(1)}) fusion(f32[4,12,96,384]{3,2,1,0:T(8,128)} %convolution_bitcast_fusion.2, f32[4,12,96,384]{3,2,1,0:T(8,128)S(1)} %convolution_bitcast_fusion.3), kind=kLoop, calls=%fused_computation.13 | loop fusion | flops 3538944 | bytes 17694720 | tf_op jit(solution)/shard_map/convert
  206.7 1.3 pad_maximum_fusion.1
  208.0 4.5 %copy.75 = bf16[4,12,96,384]{3,0,1,2:T(4,128)(2,1)} copy(bf16[4,12,96,384]{3,2,1,0:T(8,128)(2,1)S(1)} %pad_maximum_fusion.1) | data formatting | bytes 7077888 | tf_op jit(solution)/shard_map/concatenate | solution.py:42
  212.5 5.6 %all-to-all-start.1 = ((bf16[4,12,96,384]{3,0,1,2:T(4,128)(2,1)}), bf16[4,12,96,384]{3,0,1,2:T(4,128)(2,1)S(1)}, u32[]{:S(2)}, u32[]{:S(2)}) async-start(bf16[4,12,96,384]{3,0,1,2:T(4,128)(2,1)} %copy.75), calls=%async_computation.1 | async-start | bytes 7077888 | tf_op jit(solution)/shard_map/all_to_all | solution.py:115
  224.4 75.5 %all-to-all-done.1 = bf16[4,12,96,384]{3,0,1,2:T(4,128)(2,1)S(1)} async-done(((bf16[4,12,96,384]{3,0,1,2:T(4,128)(2,1)}), bf16[4,12,96,384]{3,0,1,2:T(4,128)(2,1)S(1)}, u32[]{:S(2)}, u32[]{:S(2)}) %all-to-all-start.1) | async-done | bytes 3538976 | tf_op jit(solution)/shard_map/all_to_all | solution.py:115
  301.1 1.5 fusion.14
  306.7 3.0 fusion.13
  309.7 3.2 %gather_fusion.1 = bf16[576,4,192]{2,1,0:T(4,128)(2,1)S(1)} fusion(bf16[4,576,192]{2,0,1:T(4,128)(2,1)S(1)} %fusion.13, s32[1024]{0:T(1024)S(1)} %pad_clamp_fusion), kind=kCustom, calls=%fused_computation.1.clone | custom fusion | bytes 1771776 | tf_op jit(solution)/shard_map/jit(_take)/gather | solution.py:122
  313.0 2.1 select_bitcast_fusion
  315.1 2.2 copy.81
  (65 shorter events, 24.4 us)
Async XLA Ops:
  1.8 10.1 %collective-permute-start = (bf16[2,576,192]{1,0,2:T(2,128)(2,1)S(1)}, bf16[2,576,192]{1,0,2:T(2,128)(2,1)S(1)}, u32[]{:S(2)}, u32[]{:S(2)}) collective-permute-start(bf16[2,576,192]{1,0,2:T(2,128)(2,1)S(1)} %copy.97), channel_id=1, source_target_pairs={{0,16},{16,32},{32,48},{48,64},{64,80},{80,96},{96,112},{112,128},... | collective-permute-start | bytes 1327112 | tf_op jit(solution)/shard_map/ppermute | solution.py:16
  5.4 9.7 %copy-start.9 = (s32[576]{0:T(1024)}, s32[576]{0:T(1024)S(1)}, u32[]{:S(2)}) copy-start(s32[576]{0:T(1024)S(1)} %compare_select_fusion) | copy-start | bytes 6916
  9.5 61.3 %copy-start.10 = (pred[576]{0:T(1024)(128)(4,1)}, pred[576]{0:T(1024)(128)(4,1)S(1)}, u32[]{:S(2)}) copy-start(pred[576]{0:T(1024)(128)(4,1)S(1)} %compare_and_fusion.1) | copy-start | bytes 1732
  13.7 46.4 %copy-start.13 = (s32[1,2,2]{2,1,0:T(2,128)S(1)}, s32[1,2,2]{2,1,0:T(2,128)}, u32[]{:S(2)}) copy-start(s32[1,2,2]{2,1,0:T(2,128)} %param.8) | copy-start | bytes 52
  70.8 2.2 copy-start.2
  84.5 80.2 %all-to-all-start = ((bf16[4,192,6,384]{3,0,2,1:T(4,128)(2,1)}), bf16[4,192,6,384]{3,0,2,1:T(4,128)(2,1)S(1)}, u32[]{:S(2)}, u32[]{:S(2)}) async-start(bf16[4,192,6,384]{3,0,2,1:T(4,128)(2,1)} %copy.69), calls=%async_computation | async-start | bytes 7077888 | tf_op jit(solution)/shard_map/all_to_all | solution.py:108
  188.1 6.8 %copy-start = (bf16[4,12,192,192]{3,2,1,0:T(8,128)(2,1)S(1)}, bf16[4,12,192,192]{3,2,1,0:T(8,128)(2,1)}, u32[]{:S(2)}) copy-start(bf16[4,12,192,192]{3,2,1,0:T(8,128)(2,1)} %get-tuple-element.10) | copy-start | bytes 10616836
  188.2 6.8 %copy-start.1 = (f32[12,192,384]{2,1,0:T(8,128)S(1)}, f32[12,192,384]{2,1,0:T(8,128)}, u32[]{:S(2)}) copy-start(f32[12,192,384]{2,1,0:T(8,128)} %pad_maximum_fusion) | copy-start | bytes 10616836
  212.5 8.1 %copy-start.8 = (s32[576]{0:T(1024)S(1)}, s32[576]{0:T(1024)}, u32[]{:S(2)}) copy-start(s32[576]{0:T(1024)} %param.9) | copy-start | bytes 6916
  212.5 87.3 %all-to-all-start.1 = ((bf16[4,12,96,384]{3,0,1,2:T(4,128)(2,1)}), bf16[4,12,96,384]{3,0,1,2:T(4,128)(2,1)S(1)}, u32[]{:S(2)}, u32[]{:S(2)}) async-start(bf16[4,12,96,384]{3,0,1,2:T(4,128)(2,1)} %copy.75), calls=%async_computation.1 | async-start | bytes 7077888 | tf_op jit(solution)/shard_map/all_to_all | solution.py:115
  299.8 1.2 copy-start.5
  299.8 1.2 copy-start.6
  299.8 1.2 copy-start.7
  305.1 1.6 copy-start.3
  305.1 1.6 copy-start.4
  305.1 1.6 copy-start.11
  306.7 6.3 %copy-start.12 = (pred[576]{0:T(1024)(128)(4,1)S(1)}, pred[576]{0:T(1024)(128)(4,1)}, u32[]{:S(2)}) copy-start(pred[576]{0:T(1024)(128)(4,1)} %compare_and_fusion) | copy-start | bytes 1732
where the time goes:
time: 322 us; the launch traced here: 318 us
  waiting for transfers between devices  148 us (46%)
  blocking collectives  44.3 us (14%)
  other arithmetic  43.1 us (13%)
  matrix products  36.3 us (11%)
  local copies, waits for them, and re-layouts  33.5 us (10%)
  starting transfers between devices  11.8 us (4%)
    all_to_all x1, waiting for transfers between devices, local(): lax.all_to_all(back_one, 'pencil', split_axis=2, concat_axis=1, tiled=True)  75.5 us
    all_to_all x1, waiting for transfers between devices, local(): lax.all_to_all(section_two, 'pencil', split_axis=1, concat_axis=2, tiled=...  71 us
    psum x1, blocking collectives, local(): lax.psum((correlation_real, correlation_imag, neighbor_norms), 'pencil')  44.3 us
    another operation x3, other arithmetic  18.6 us
    dot_general x3, matrix products, along_axis(): jnp.einsum(pattern, values, sin_table, preferred_element_type=jnp.float32)  14.8 us
    dot_general x3, matrix products, along_axis(): jnp.einsum(pattern, values, cos_table, preferred_element_type=jnp.float32)  10.2 us
  transfers between devices with their start and end apart: 3, of which 3 were waited for; matrix products, arithmetic and copies ran while one was open for 6% of the time, Pallas kernels for 0%

commit v1 on v0

v1 whole, which is shorter than its diff:
```python
import math

import jax
import jax.numpy as jnp
import ml_dtypes
import numpy as np
from jax import lax
from jax.experimental import pallas as pl
from jax.experimental.pallas import tpu as pltpu
from jax.sharding import PartitionSpec as P

GRID = 192
EDGE = 2
GBOX = 96
PENCILS = 16
X_DEV = GRID // PENCILS
GY_DEV = GBOX // PENCILS
STICKS_DEV = GBOX * GY_DEV
WIDTH = 2 * GBOX
CHUNK = X_DEV * GY_DEV
ROWS = PENCILS * CHUNK
LANES = EDGE * WIDTH
BLOCK = 4 * CHUNK
STATS = 16

bf16 = jnp.bfloat16
f32 = jnp.float32
NT = (((1,), (1,)), ((), ()))
TN = (((0,), (0,)), ((), ()))
VMEM = pltpu.VMEM


def tables():
    phases = 2.0 * np.pi / GRID * np.mod(np.outer(np.arange(GBOX) - GBOX // 2, np.arange(GRID)), GRID)
    scale = 1.0 / math.sqrt(GBOX)
    rounded = lambda a: a.astype(np.float32).astype(ml_dtypes.bfloat16).astype(np.float64)
    return rounded(np.cos(phases) * scale), rounded(np.sin(phases) * scale)


def constants():
    cos, sin = tables()
    low = lambda a: np.asarray(a, np.float32).astype(ml_dtypes.bfloat16)
    order = (np.arange(PENCILS)[:, None, None] * X_DEV + np.zeros((1, GY_DEV, 1), int) + np.arange(X_DEV)[None, None, :]).reshape(-1)
    first = np.concatenate([cos.T[order], sin.T[order]], axis=0)
    core = np.zeros((WIDTH, 512))
    core[:GBOX, :GRID] = cos
    core[GBOX:, :GRID] = -sin
    core[:GBOX, 256 : 256 + GRID] = sin
    core[GBOX:, 256 : 256 + GRID] = cos
    third = np.zeros((2, 256, 512))
    third[0, :WIDTH] = core
    third[1, 64:] = core
    second = np.block([[cos.T, -sin.T], [sin.T, cos.T]])
    back_second = 0.5 * np.block([[cos, sin], [-sin, cos]])
    back = 0.5 * np.block([[cos.T, -sin.T], [sin.T, cos.T]])
    back_third = np.zeros((2, 2 * GRID, 256))
    back_third[0, :, :WIDTH] = back
    back_third[1, :, 64:] = back
    return [low(a) for a in (first, third, second, back_second, back_third)]


def dot(a, b, dims=None):
    if dims is None:
        return jnp.dot(a, b, preferred_element_type=f32)
    return lax.dot_general(a, b, dims, preferred_element_type=f32)


def whole(*_):
    return pl.BlockSpec(memory_space=VMEM)


def sixth(value):
    return (value * 10923) >> 16


def matrix_kernel(map_ref, first_ref, cos_ref, sin_ref):
    position = map_ref[...]
    kx = sixth(position)
    ky = position - GY_DEV * kx
    select = (lax.broadcasted_iota(jnp.int32, (GBOX, STICKS_DEV), 0) == kx).astype(f32).astype(bf16)
    row = lax.broadcasted_iota(jnp.int32, (CHUNK, STICKS_DEV), 0)
    row_ky = (row * 5462) >> 16
    mask = row_ky == ky
    for part in range(2):
        out_ref = (cos_ref, sin_ref)[part]
        for b in range(PENCILS):
            spread = dot(first_ref[pl.ds(part * ROWS + b * CHUNK, CHUNK), :], select)
            out_ref[pl.ds(b * CHUNK, CHUNK), :] = jnp.where(mask, spread, 0.0).astype(bf16)


def build_matrix(position, first):
    shape = jax.ShapeDtypeStruct((ROWS, STICKS_DEV), bf16)
    return pl.pallas_call(
        matrix_kernel,
        out_shape=(shape, shape),
        in_specs=[whole(), whole()],
        out_specs=(whole(), whole()),
        name="matrix",
    )(position, first)


def stats_kernel(upper_ref, lower_ref, out_ref):
    def total(a, b):
        return jnp.sum(a * b)

    rows = lax.broadcasted_iota(jnp.int32, (STATS, 128), 0)
    out = jnp.zeros((STATS, 128), f32)
    for j in range(EDGE):
        p_re = upper_ref[j, :GBOX, :].astype(f32)
        p_im = upper_ref[j, GBOX:, :].astype(f32)
        for i in range(EDGE):
            u_re = lower_ref[i, :GBOX, :].astype(f32)
            u_im = lower_ref[i, GBOX:, :].astype(f32)
            real = jnp.sum(p_re * u_re + p_im * u_im)
            imag = jnp.sum(p_re * u_im - p_im * u_re)
            out = jnp.where(rows == 2 * j + i, real, out)
            out = jnp.where(rows == 4 + 2 * j + i, imag, out)
        out = jnp.where(rows == 8 + j, jnp.sum(p_re * p_re + p_im * p_im), out)
    out_ref[...] = out


def stats(upper, lower):
    return pl.pallas_call(
        stats_kernel,
        out_shape=jax.ShapeDtypeStruct((STATS, 128), f32),
        in_specs=[whole(), whole()],
        out_specs=whole(),
        name="stats",
    )(upper, lower)


def spread_rows(bands, cos_ref, sin_ref, out_ref):
    plain = jnp.concatenate([part for re, im in bands for part in (re, im)], axis=0)
    turned = jnp.concatenate([part for re, im in bands for part in (-im, re)], axis=0)
    for b in range(0, ROWS, BLOCK):
        rows = pl.ds(b, BLOCK)
        out_ref[rows, :] = (dot(cos_ref[rows, :], plain, NT) + dot(sin_ref[rows, :], turned, NT)).astype(bf16)


def ahead_kernel(bands_ref, cos_ref, sin_ref, out_ref):
    spread_rows([(bands_ref[b, :GBOX, :], bands_ref[b, GBOX:, :]) for b in range(EDGE)], cos_ref, sin_ref, out_ref)


def ahead(bands, cos, sin):
    return pl.pallas_call(
        ahead_kernel,
        out_shape=jax.ShapeDtypeStruct((ROWS, LANES), bf16),
        grid=(1,),
        in_specs=[pl.BlockSpec((EDGE, WIDTH, STICKS_DEV), lambda i: (1, 0, 0)), whole(), whole()],
        out_specs=whole(),
        name="ahead",
    )(bands, cos, sin)


def edge_kernel(keep_ref, total_ref, bands_ref, upper_ref, cos_ref, sin_ref, out_ref, ortho_ref):
    bands = []
    for i in range(EDGE):
        u_re = bands_ref[i, :GBOX, :].astype(f32)
        u_im = bands_ref[i, GBOX:, :].astype(f32)
        for j in range(EDGE):
            keep = keep_ref[0, i, j].astype(f32)
            divisor = total_ref[8 + j : 9 + j, 0:1] + 1e-05
            w_re = keep * total_ref[2 * j + i : 2 * j + i + 1, 0:1] / divisor
            w_im = keep * total_ref[4 + 2 * j + i : 5 + 2 * j + i, 0:1] / divisor
            p_re = upper_ref[j, :GBOX, :].astype(f32)
            p_im = upper_ref[j, GBOX:, :].astype(f32)
            u_re = u_re - (w_re * p_re - w_im * p_im)
            u_im = u_im - (w_re * p_im + w_im * p_re)
        re, im = u_re.astype(bf16), u_im.astype(bf16)
        ortho_ref[i, :GBOX, :] = re
        ortho_ref[i, GBOX:, :] = im
        bands.append((re, im))
    spread_rows(bands, cos_ref, sin_ref, out_ref)


def edge_ahead(keep, total, bands, upper, cos, sin):
    return pl.pallas_call(
        edge_kernel,
        out_shape=(
            jax.ShapeDtypeStruct((ROWS, LANES), bf16),
            jax.ShapeDtypeStruct((EDGE, WIDTH, STICKS_DEV), bf16),
        ),
        grid=(1,),
        in_specs=[
            pl.BlockSpec(memory_space=pltpu.SMEM),
            whole(),
            pl.BlockSpec((EDGE, WIDTH, STICKS_DEV), lambda i: (0, 0, 0)),
            whole(),
            whole(),
            whole(),
        ],
        out_specs=(whole(), whole()),
        name="edge",
    )(keep, total, bands, upper, cos, sin)


def grid_kernel(rows_ref, potential_ref, third_ref, second_ref, back_second_ref, back_third_ref, out_ref, wide_ref, back_ref):
    for t in range(3):
        wide_ref[t] = rows_ref[:, 128 * t : 128 * t + 128].astype(f32)

    def plane(x, carry):
        rows = pl.ds(x, GBOX, stride=X_DEV)
        section = jnp.concatenate([wide_ref[t, rows, :] for t in range(3)], axis=1).astype(bf16)
        field = potential_ref[x]
        results = []
        for b in range(EDGE):
            lanes = section[:, 128 * b : 128 * b + 256]
            two = dot(lanes, third_ref[b]).astype(bf16)
            stacked = jnp.concatenate([two[:, :GRID], two[:, 256 : 256 + GRID]], axis=0)
            space = dot(second_ref[...], stacked)
            scaled = jnp.concatenate([space[:GRID] * field, space[GRID:] * field], axis=0).astype(bf16)
            one = dot(back_second_ref[...], scaled).astype(bf16)
            results.append(dot(one[:GBOX], back_third_ref[b, :GRID, :]) + dot(one[GBOX:], back_third_ref[b, GRID:, :]))
        back_ref[0, rows, :] = results[0][:, :128]
        back_ref[1, rows, :] = results[0][:, 128:] + results[1][:, :128]
        back_ref[2, rows, :] = results[1][:, 128:]
        return carry

    lax.fori_loop(0, X_DEV, plane, 0)
    for t in range(3):
        out_ref[:, 128 * t : 128 * t + 128] = back_ref[t].astype(bf16)


def on_grid(rows, potential, consts):
    third, second, back_second, back_third = consts
    flops = 2 * EDGE * X_DEV * (96 * 256 * 512 + 384 * 256 * 256 * 2 + 96 * 512 * 256)
    return pl.pallas_call(
        grid_kernel,
        out_shape=jax.ShapeDtypeStruct((ROWS, LANES), bf16),
        in_specs=[whole()] * 6,
        out_specs=whole(),
        scratch_shapes=[VMEM((3, ROWS, 128), f32), VMEM((3, ROWS, 128), f32)],
        cost_estimate=pl.CostEstimate(flops=flops, bytes_accessed=8_000_000, transcendentals=0),
        name="grid",
    )(rows, potential, third, second, back_second, back_third)


def behind_kernel(map_ref, across_ref, rows_ref, cos_ref, sin_ref, bands_ref, out_ref):
    position = map_ref[...]
    kx = sixth(position)
    gx = (kx - GBOX // 2).astype(f32)
    gy = (position - GY_DEV * kx + GY_DEV * across_ref[0] - GBOX // 2).astype(f32)
    gz = (lax.broadcasted_iota(jnp.int32, (GBOX, STICKS_DEV), 0) - GBOX // 2).astype(f32)
    kinetic = 0.5 * (gx * gx + gy * gy + gz * gz) / float((GBOX // 2) ** 2)
    rows = rows_ref[...]
    by_cos = dot(rows, cos_ref[...], TN)
    by_sin = dot(rows, sin_ref[...], TN)
    for b in range(EDGE):
        re = slice(b * WIDTH, b * WIDTH + GBOX)
        im = slice(b * WIDTH + GBOX, (b + 1) * WIDTH)
        out_ref[b, :GBOX, :] = (0.5 * (by_cos[re] + by_sin[im]) + kinetic * bands_ref[b, :GBOX, :].astype(f32)).astype(bf16)
        out_ref[b, GBOX:, :] = (0.5 * (by_cos[im] - by_sin[re]) + kinetic * bands_ref[b, GBOX:, :].astype(f32)).astype(bf16)


def behind(position, across, rows, cos, sin, bands, index):
    return pl.pallas_call(
        behind_kernel,
        out_shape=jax.ShapeDtypeStruct((EDGE, WIDTH, STICKS_DEV), bf16),
        grid=(1,),
        in_specs=[
            whole(),
            pl.BlockSpec(memory_space=pltpu.SMEM),
            whole(),
            whole(),
            whole(),
            pl.BlockSpec((EDGE, WIDTH, STICKS_DEV), lambda i: (index, 0, 0)),
        ],
        out_specs=whole(),
        name="behind",
    )(position, across, rows, cos, sin, bands)


def exchange(rows):
    blocks = rows.reshape(PENCILS, CHUNK, LANES)
    return lax.all_to_all(blocks, "pencil", split_axis=0, concat_axis=0, tiled=True).reshape(ROWS, LANES)


def total_over_pencil(value):
    for bit in (2, 4, 8, 1):
        value = value + lax.ppermute(value, "pencil", [(i, i ^ bit) for i in range(PENCILS)])
    return value


def local(wavefunctions, potential, keep_mask, stick_map):
    first, *grid_consts = [jnp.asarray(c) for c in constants()]
    bands = jnp.transpose(wavefunctions, (0, 2, 1))
    slices = lax.axis_size("cuts")
    upper = lax.ppermute(bands[EDGE:], "cuts", [(i, i + 1) for i in range(slices - 1)])
    position = stick_map.reshape(1, STICKS_DEV)
    cos, sin = build_matrix(position, first)
    inner_rows = exchange(ahead(bands, cos, sin))
    total = total_over_pencil(stats(upper, bands[:EDGE]))
    edge_rows, ortho = edge_ahead(keep_mask, total, bands, upper, cos, sin)
    edge_rows = exchange(edge_rows)
    inner_back = exchange(on_grid(inner_rows, potential, grid_consts))
    edge_back = exchange(on_grid(edge_rows, potential, grid_consts))
    across = lax.axis_index("pencil").reshape(1).astype(jnp.int32)
    inner_out = behind(position, across, inner_back, cos, sin, bands, 1)
    edge_out = behind(position, across, edge_back, cos, sin, ortho, 0)
    return jnp.transpose(jnp.concatenate([edge_out, inner_out], axis=0), (0, 2, 1))


def solution(mesh):
    return jax.shard_map(
        local,
        mesh=mesh,
        in_specs=(
            P("cuts", "pencil", None),
            P("pencil", None, None),
            P("cuts", None, None),
            P("pencil"),
        ),
        out_specs=P("cuts", "pencil", None),
        check_vma=False,
    )
```

time: 322 us -> 160 us (0.50); the launches traced: 318 us -> 160 us
  waiting for transfers between devices: 148 us -> 44.3 us
  Pallas kernels: 0 us -> 60.5 us
  blocking collectives: 44.3 us -> 0 us
  other arithmetic: 43.1 us -> 3.41 us
  matrix products: 36.3 us -> 0 us
  starting transfers between devices: 11.8 us -> 47.4 us
  local copies, waits for them, and re-layouts: 33.5 us -> 3.87 us
    all_to_all x2 -> x4, waiting for transfers between devices: 146 us -> 26.2 us  [exchange(): lax.all_to_all(blocks, 'pencil', split_axis=0, concat_axis=0, tiled=True)]
    pallas_call x0 -> x8, Pallas kernels: none -> 60.5 us  [the longest x2 35.4 us: on_grid(): pl.pallas_call(grid_kernel, out_shape=jax.ShapeDtypeStruct((ROWS, LANES),...]
    psum x1 -> x0, blocking collectives: 44.3 us -> none  [local(): lax.psum((correlation_real, correlation_imag, neighbor_norms), 'pencil')]
    dot_general x13 -> x0, matrix products: 33.9 us -> none  [the longest x3 14.8 us: along_axis(): jnp.einsum(pattern, values, sin_table, preferred_element_type=jnp.float32)]
    all_to_all x2 -> x4, starting transfers between devices: 9.93 us -> 31.1 us  [exchange(): lax.all_to_all(blocks, 'pencil', split_axis=0, concat_axis=0, tiled=True)]
    another operation x3 -> x0, other arithmetic: 18.6 us -> none
    ppermute x1 -> x5, waiting for transfers between devices: 1.29 us -> 18.1 us  [the longest x4 9.31 us: total_over_pencil(): lax.ppermute(value, 'pencil', [(i, i ^ bit) for i in range(PENCILS)])]
    ppermute x1 -> x5, starting transfers between devices: 1.92 us -> 16.3 us  [the longest x4 14.4 us: total_over_pencil(): lax.ppermute(value, 'pencil', [(i, i ^ bit) for i in range(PENCILS)])]
  transfers between devices with their start and end apart: 3 -> 9, of which waited for: 3 -> 8; matrix products, arithmetic and copies ran while one was open for 6% -> 1% of each run, Pallas kernels for 0% -> 30%
where the time goes in v1:
time: 160 us
  Pallas kernels  60.5 us (38%)
  starting transfers between devices  47.4 us (30%)
  waiting for transfers between devices  44.3 us (28%)
  local copies, waits for them, and re-layouts  3.87 us (2%)
  other arithmetic  3.41 us (2%)
    pallas_call x2, Pallas kernels, on_grid(): pl.pallas_call(grid_kernel, out_shape=jax.ShapeDtypeStruct((ROWS, LANES),...  35.4 us
    all_to_all x4, starting transfers between devices, exchange(): lax.all_to_all(blocks, 'pencil', split_axis=0, concat_axis=0, tiled=True)  31.1 us
    all_to_all x4, waiting for transfers between devices, exchange(): lax.all_to_all(blocks, 'pencil', split_axis=0, concat_axis=0, tiled=True)  26.2 us
    ppermute x4, starting transfers between devices, total_over_pencil(): lax.ppermute(value, 'pencil', [(i, i ^ bit) for i in range(PENCILS)])  14.4 us
    pallas_call x2, Pallas kernels, behind(): pl.pallas_call(behind_kernel, out_shape=jax.ShapeDtypeStruct((EDGE, WIDTH...  9.36 us
    ppermute x4, waiting for transfers between devices, total_over_pencil(): lax.ppermute(value, 'pencil', [(i, i ^ bit) for i in range(PENCILS)])  9.31 us
    ppermute x1, waiting for transfers between devices, local(): lax.ppermute(bands[EDGE:], 'cuts', [(i, i + 1) for i in range(slices - 1)])  8.81 us
    pallas_call x1, Pallas kernels, edge_ahead(): pl.pallas_call(edge_kernel, out_shape=(jax.ShapeDtypeStruct((ROWS, LANES)...  5.28 us
  transfers between devices with their start and end apart: 9, of which 8 were waited for; matrix products, arithmetic and copies ran while one was open for 1% of the time, Pallas kernels for 30%

profile of v1, /device:TPU:10, one launch (start us, length us, event | category | flops | bytes accessed | tf_op | source)
XLA Modules:
  0.0 159.6 jit_solution(4596337990029833474)
XLA Ops:
  0.0 1.3 reshape.30.map_ref
  1.3 3.4 %matrix.1 = (bf16[1152,576]{1,0:T(8,128)(2,1)}, bf16[1152,576]{1,0:T(8,128)(2,1)}) custom-call(s32[1,576]{1,0:T(1,128)} %reshape.30.map_ref, bf16[2304,96]{1,0:T(8,128)(2,1)} %constant.14.clone.first_ref), custom_call_target="tpu_custom_call" | custom-call | tf_op jit(solution)/shard_map/matrix/pallas_call | solution.py:93
  4.7 4.8 %ahead.1 = bf16[1152,384]{1,0:T(8,128)(2,1)} custom-call(bf16[4,192,576]{2,1,0:T(8,128)(2,1)} %bitcast.12, bf16[1152,576]{1,0:T(8,128)(2,1)} %get-tuple-element.9.cos_ref, bf16[1152,576]{1,0:T(8,128)(2,1)} %get-tuple-element.10.sin_ref), custom_call_target="tpu_custom_call" | custom-call | tf_op jit(solution)/shard_map/ahead/pallas_call | solution.py:145
  9.4 10.3 %all-to-all-start.2 = ((bf16[16,72,384]{2,1,0:T(8,128)(2,1)}), bf16[16,72,384]{2,1,0:T(8,128)(2,1)S(1)}, u32[]{:S(2)}, u32[]{:S(2)}) async-start(bf16[16,72,384]{2,1,0:T(8,128)(2,1)} %bitcast.16), calls=%async_computation.2 | async-start | bytes 1769472 | tf_op jit(solution)/shard_map/all_to_all | solution.py:275
  19.7 0.9 fusion
  20.6 1.9 %collective-permute-start = (bf16[2,192,576]{2,1,0:T(8,128)(2,1)S(1)}, bf16[2,192,576]{2,1,0:T(8,128)(2,1)S(1)}, u32[]{:S(2)}, u32[]{:S(2)}) collective-permute-start(bf16[2,192,576]{2,1,0:T(8,128)(2,1)S(1)} %get-tuple-element.14), channel_id=1, source_target_pairs={{0,16},{16,32},{32,48},{48,64},{64,80},{80,96},{96,112},{112,128},... | collective-permute-start | bytes 1327112 | tf_op jit(solution)/shard_map/ppermute | solution.py:288
  22.5 8.8 %collective-permute-done.upper_ref = bf16[2,192,576]{2,1,0:T(8,128)(2,1)S(1)} collective-permute-done((bf16[2,192,576]{2,1,0:T(8,128)(2,1)S(1)}, bf16[2,192,576]{2,1,0:T(8,128)(2,1)S(1)}, u32[]{:S(2)}, u32[]{:S(2)}) %collective-permute-start) | collective-permute-done | bytes 442400 | tf_op jit(solution)/shard_map/ppermute | solution.py:288
  31.3 0.8 copy-done.3
  32.1 2.4 %stats.1 = f32[16,128]{1,0:T(8,128)} custom-call(bf16[2,192,576]{2,1,0:T(8,128)(2,1)} %copy-done.3, bf16[2,192,576]{2,1,0:T(8,128)(2,1)} %get-tuple-element.13.lower_ref), custom_call_target="tpu_custom_call" | custom-call | tf_op jit(solution)/shard_map/stats/pallas_call | solution.py:123
  34.5 2.8 %collective-permute-start.1 = (f32[16,128]{1,0:T(8,128)}, f32[16,128]{1,0:T(8,128)S(1)}, u32[]{:S(2)}, u32[]{:S(2)}) collective-permute-start(f32[16,128]{1,0:T(8,128)} %stats.1), channel_id=1, source_target_pairs={{0,2},{1,3},{2,0},{3,1},{4,6},{5,7},{6,4},{7,5},{8,10},{9,11},{10,... | collective-permute-start | bytes 24584 | tf_op jit(solution)/shard_map/ppermute | solution.py:280
  37.3 3.3 %collective-permute-done.1 = f32[16,128]{1,0:T(8,128)S(1)} collective-permute-done((f32[16,128]{1,0:T(8,128)}, f32[16,128]{1,0:T(8,128)S(1)}, u32[]{:S(2)}, u32[]{:S(2)}) %collective-permute-start.1) | collective-permute-done | bytes 8224 | tf_op jit(solution)/shard_map/ppermute | solution.py:280
  40.6 0.7 add.12
  41.3 2.8 %collective-permute-start.2 = (f32[16,128]{1,0:T(8,128)S(1)}, f32[16,128]{1,0:T(8,128)S(1)}, u32[]{:S(2)}, u32[]{:S(2)}) collective-permute-start(f32[16,128]{1,0:T(8,128)S(1)} %add.12), channel_id=1, source_target_pairs={{0,4},{1,5},{2,6},{3,7},{4,0},{5,1},{6,2},{7,3},{8,12},{9,13},{10,... | collective-permute-start | bytes 24584 | tf_op jit(solution)/shard_map/ppermute | solution.py:280
  44.1 1.7 %collective-permute-done.2 = f32[16,128]{1,0:T(8,128)S(1)} collective-permute-done((f32[16,128]{1,0:T(8,128)S(1)}, f32[16,128]{1,0:T(8,128)S(1)}, u32[]{:S(2)}, u32[]{:S(2)}) %collective-permute-start.2) | collective-permute-done | bytes 8224 | tf_op jit(solution)/shard_map/ppermute | solution.py:280
  45.8 4.9 %collective-permute-start.3 = (f32[16,128]{1,0:T(8,128)S(1)}, f32[16,128]{1,0:T(8,128)S(1)}, u32[]{:S(2)}, u32[]{:S(2)}) collective-permute-start(f32[16,128]{1,0:T(8,128)S(1)} %add.13), channel_id=1, source_target_pairs={{0,8},{1,9},{2,10},{3,11},{4,12},{5,13},{6,14},{7,15},{8,0},{9,1},... | collective-permute-start | bytes 24584 | tf_op jit(solution)/shard_map/ppermute | solution.py:280
  50.8 2.6 %collective-permute-done.3 = f32[16,128]{1,0:T(8,128)S(1)} collective-permute-done((f32[16,128]{1,0:T(8,128)S(1)}, f32[16,128]{1,0:T(8,128)S(1)}, u32[]{:S(2)}, u32[]{:S(2)}) %collective-permute-start.3) | collective-permute-done | bytes 8224 | tf_op jit(solution)/shard_map/ppermute | solution.py:280
  53.4 3.8 %collective-permute-start.4 = (f32[16,128]{1,0:T(8,128)S(1)}, f32[16,128]{1,0:T(8,128)S(1)}, u32[]{:S(2)}, u32[]{:S(2)}) collective-permute-start(f32[16,128]{1,0:T(8,128)S(1)} %add.14), channel_id=1, source_target_pairs={{0,1},{1,0},{2,3},{3,2},{4,5},{5,4},{6,7},{7,6},{8,9},{9,8},{10,11... | collective-permute-start | bytes 24584 | tf_op jit(solution)/shard_map/ppermute | solution.py:280
  57.2 1.6 %collective-permute-done.4 = f32[16,128]{1,0:T(8,128)S(1)} collective-permute-done((f32[16,128]{1,0:T(8,128)S(1)}, f32[16,128]{1,0:T(8,128)S(1)}, u32[]{:S(2)}, u32[]{:S(2)}) %collective-permute-start.4) | collective-permute-done | bytes 8224 | tf_op jit(solution)/shard_map/ppermute | solution.py:280
  58.9 0.6 add.15.total_ref
  59.5 5.3 %edge.1 = (bf16[1152,384]{1,0:T(8,128)(2,1)}, bf16[2,192,576]{2,1,0:T(8,128)(2,1)}) custom-call(s32[1,2,2]{2,1,0:T(2,128)} %keep_ref.1, f32[16,128]{1,0:T(8,128)} %add.15.total_ref, bf16[4,192,576]{2,1,0:T(8,128)(2,1)} %bitcast.13, bf16[2,192,576]{2,1,0:T(8,128)(2,1)} %copy-done.3, bf16[1152,576]{1,0:T(8,128)(2,1)} %get-tuple-element.9.cos_ref, ...), custom_call_target="tpu_custom_call" | custom-call | tf_op jit(solution)/shard_map/edge/pallas_call | solution.py:177
  64.8 10.7 %all-to-all-start = ((bf16[16,72,384]{2,1,0:T(8,128)(2,1)}), bf16[16,72,384]{2,1,0:T(8,128)(2,1)S(1)}, u32[]{:S(2)}, u32[]{:S(2)}) async-start(bf16[16,72,384]{2,1,0:T(8,128)(2,1)} %bitcast.23), calls=%async_computation | async-start | bytes 1769472 | tf_op jit(solution)/shard_map/all_to_all | solution.py:275
  75.5 17.7 %grid.3 = bf16[1152,384]{1,0:T(8,128)(2,1)} custom-call(bf16[1152,384]{1,0:T(8,128)(2,1)} %bitcast.19, f32[12,192,192]{2,1,0:T(8,128)} %potential_ref.3, bf16[2,256,512]{2,1,0:T(8,128)(2,1)} %constant.15.clone.third_ref, bf16[384,192]{1,0:T(8,128)(2,1)} %constant.16.clone.second_ref, bf16[192,384]{1,0:T(8,128)(2,1)} %constant.17.clone.back_second_ref, ...), custom_call_target="tpu_custom_call" | custom-call | flops 3623878656 | bytes 8000000 | tf_op jit(solution)/shard_map/grid/pallas_call | solution.py:227
  93.2 4.8 %all-to-all-done = bf16[16,72,384]{2,1,0:T(8,128)(2,1)S(1)} async-done(((bf16[16,72,384]{2,1,0:T(8,128)(2,1)}), bf16[16,72,384]{2,1,0:T(8,128)(2,1)S(1)}, u32[]{:S(2)}, u32[]{:S(2)}) %all-to-all-start) | async-done | bytes 884768 | tf_op jit(solution)/shard_map/all_to_all | solution.py:275
  98.0 4.8 %all-to-all-start.3 = ((bf16[16,72,384]{2,1,0:T(8,128)(2,1)}), bf16[16,72,384]{2,1,0:T(8,128)(2,1)S(1)}, u32[]{:S(2)}, u32[]{:S(2)}) async-start(bf16[16,72,384]{2,1,0:T(8,128)(2,1)} %bitcast.22), calls=%async_computation.3 | async-start | bytes 1769472 | tf_op jit(solution)/shard_map/all_to_all | solution.py:275
  102.8 17.7 %grid.2 = bf16[1152,384]{1,0:T(8,128)(2,1)} custom-call(bf16[1152,384]{1,0:T(8,128)(2,1)} %bitcast.21, f32[12,192,192]{2,1,0:T(8,128)} %potential_ref.3, bf16[2,256,512]{2,1,0:T(8,128)(2,1)} %constant.15.clone.third_ref, bf16[384,192]{1,0:T(8,128)(2,1)} %constant.16.clone.second_ref, bf16[192,384]{1,0:T(8,128)(2,1)} %constant.17.clone.back_second_ref, ...), custom_call_target="tpu_custom_call" | custom-call | flops 3623878656 | bytes 8000000 | tf_op jit(solution)/shard_map/grid/pallas_call | solution.py:227
  120.5 4.3 %all-to-all-done.3 = bf16[16,72,384]{2,1,0:T(8,128)(2,1)S(1)} async-done(((bf16[16,72,384]{2,1,0:T(8,128)(2,1)}), bf16[16,72,384]{2,1,0:T(8,128)(2,1)S(1)}, u32[]{:S(2)}, u32[]{:S(2)}) %all-to-all-start.3) | async-done | bytes 884768 | tf_op jit(solution)/shard_map/all_to_all | solution.py:275
  124.8 5.3 %all-to-all-start.1 = ((bf16[16,72,384]{2,1,0:T(8,128)(2,1)}), bf16[16,72,384]{2,1,0:T(8,128)(2,1)S(1)}, u32[]{:S(2)}, u32[]{:S(2)}) async-start(bf16[16,72,384]{2,1,0:T(8,128)(2,1)} %bitcast.20), calls=%async_computation.1 | async-start | bytes 1769472 | tf_op jit(solution)/shard_map/all_to_all | solution.py:275
  130.2 4.7 %behind.3 = bf16[2,192,576]{2,1,0:T(8,128)(2,1)} custom-call(s32[1,576]{1,0:T(1,128)} %reshape.30.map_ref, s32[1]{0:T(128)} %bitcast.across_ref, bf16[1152,384]{1,0:T(8,128)(2,1)} %bitcast.18, bf16[1152,576]{1,0:T(8,128)(2,1)} %get-tuple-element.9.cos_ref, bf16[1152,576]{1,0:T(8,128)(2,1)} %get-tuple-element.10.sin_ref, bf16[4,192,576]{2,1,0:T(8,128)(2,1)} %bitcast.14), custom_call_target="tpu_custom_call" | custom-call | tf_op jit(solution)/shard_map/behind/pallas_call | solution.py:256
  134.8 17.1 %all-to-all-done.1 = bf16[16,72,384]{2,1,0:T(8,128)(2,1)S(1)} async-done(((bf16[16,72,384]{2,1,0:T(8,128)(2,1)}), bf16[16,72,384]{2,1,0:T(8,128)(2,1)S(1)}, u32[]{:S(2)}, u32[]{:S(2)}) %all-to-all-start.1) | async-done | bytes 884768 | tf_op jit(solution)/shard_map/all_to_all | solution.py:275
  151.9 0.9 copy-done.1
  152.8 4.7 %behind.2 = bf16[2,192,576]{2,1,0:T(8,128)(2,1)} custom-call(s32[1,576]{1,0:T(1,128)} %reshape.30.map_ref, s32[1]{0:T(128)} %bitcast.across_ref, bf16[1152,384]{1,0:T(8,128)(2,1)} %bitcast.17, bf16[1152,576]{1,0:T(8,128)(2,1)} %get-tuple-element.9.cos_ref, bf16[1152,576]{1,0:T(8,128)(2,1)} %get-tuple-element.10.sin_ref, ...), custom_call_target="tpu_custom_call" | custom-call | tf_op jit(solution)/shard_map/behind/pallas_call | solution.py:256
  157.5 2.1 %maximum_bitcast_fusion = bf16[4,576,192]{1,2,0:T(8,128)(2,1)} fusion(bf16[2,192,576]{2,1,0:T(8,128)(2,1)S(1)} %copy-done.4, bf16[2,192,576]{2,1,0:T(8,128)(2,1)} %behind.2), kind=kLoop, calls=%fused_computation | loop fusion | flops 442368 | bytes 1769472 | tf_op jit(solution)/shard_map/transpose | solution.py:300
  (15 shorter events, 0.0 us)
Async XLA Ops:
  9.4 10.3 %copy-start = (bf16[4,576,192]{1,2,0:T(8,128)(2,1)S(1)}, bf16[4,576,192]{1,2,0:T(8,128)(2,1)}, u32[]{:S(2)}) copy-start(bf16[4,576,192]{1,2,0:T(8,128)(2,1)} %param.9) | copy-start | bytes 2654212
  9.4 55.3 %all-to-all-start.2 = ((bf16[16,72,384]{2,1,0:T(8,128)(2,1)}), bf16[16,72,384]{2,1,0:T(8,128)(2,1)S(1)}, u32[]{:S(2)}, u32[]{:S(2)}) async-start(bf16[16,72,384]{2,1,0:T(8,128)(2,1)} %bitcast.16), calls=%async_computation.2 | async-start | bytes 1769472 | tf_op jit(solution)/shard_map/all_to_all | solution.py:275
  20.6 10.7 %collective-permute-start = (bf16[2,192,576]{2,1,0:T(8,128)(2,1)S(1)}, bf16[2,192,576]{2,1,0:T(8,128)(2,1)S(1)}, u32[]{:S(2)}, u32[]{:S(2)}) collective-permute-start(bf16[2,192,576]{2,1,0:T(8,128)(2,1)S(1)} %get-tuple-element.14), channel_id=1, source_target_pairs={{0,16},{16,32},{32,48},{48,64},{64,80},{80,96},{96,112},{112,128},... | collective-permute-start | bytes 1327112 | tf_op jit(solution)/shard_map/ppermute | solution.py:288
  31.3 0.8 copy-start.3
  34.5 6.1 %collective-permute-start.1 = (f32[16,128]{1,0:T(8,128)}, f32[16,128]{1,0:T(8,128)S(1)}, u32[]{:S(2)}, u32[]{:S(2)}) collective-permute-start(f32[16,128]{1,0:T(8,128)} %stats.1), channel_id=1, source_target_pairs={{0,2},{1,3},{2,0},{3,1},{4,6},{5,7},{6,4},{7,5},{8,10},{9,11},{10,... | collective-permute-start | bytes 24584 | tf_op jit(solution)/shard_map/ppermute | solution.py:280
  41.3 4.5 %collective-permute-start.2 = (f32[16,128]{1,0:T(8,128)S(1)}, f32[16,128]{1,0:T(8,128)S(1)}, u32[]{:S(2)}, u32[]{:S(2)}) collective-permute-start(f32[16,128]{1,0:T(8,128)S(1)} %add.12), channel_id=1, source_target_pairs={{0,4},{1,5},{2,6},{3,7},{4,0},{5,1},{6,2},{7,3},{8,12},{9,13},{10,... | collective-permute-start | bytes 24584 | tf_op jit(solution)/shard_map/ppermute | solution.py:280
  45.8 7.6 %collective-permute-start.3 = (f32[16,128]{1,0:T(8,128)S(1)}, f32[16,128]{1,0:T(8,128)S(1)}, u32[]{:S(2)}, u32[]{:S(2)}) collective-permute-start(f32[16,128]{1,0:T(8,128)S(1)} %add.13), channel_id=1, source_target_pairs={{0,8},{1,9},{2,10},{3,11},{4,12},{5,13},{6,14},{7,15},{8,0},{9,1},... | collective-permute-start | bytes 24584 | tf_op jit(solution)/shard_map/ppermute | solution.py:280
  53.4 5.5 %collective-permute-start.4 = (f32[16,128]{1,0:T(8,128)S(1)}, f32[16,128]{1,0:T(8,128)S(1)}, u32[]{:S(2)}, u32[]{:S(2)}) collective-permute-start(f32[16,128]{1,0:T(8,128)S(1)} %add.14), channel_id=1, source_target_pairs={{0,1},{1,0},{2,3},{3,2},{4,5},{5,4},{6,7},{7,6},{8,9},{9,8},{10,11... | collective-permute-start | bytes 24584 | tf_op jit(solution)/shard_map/ppermute | solution.py:280
  64.7 10.7 %copy-start.5 = (bf16[16,72,384]{2,1,0:T(8,128)(2,1)}, bf16[16,72,384]{2,1,0:T(8,128)(2,1)S(1)}, u32[]{:S(2)}) copy-start(bf16[16,72,384]{2,1,0:T(8,128)(2,1)S(1)} %all-to-all-done.2) | copy-start | bytes 2654212
  64.8 33.2 %all-to-all-start = ((bf16[16,72,384]{2,1,0:T(8,128)(2,1)}), bf16[16,72,384]{2,1,0:T(8,128)(2,1)S(1)}, u32[]{:S(2)}, u32[]{:S(2)}) async-start(bf16[16,72,384]{2,1,0:T(8,128)(2,1)} %bitcast.23), calls=%async_computation | async-start | bytes 1769472 | tf_op jit(solution)/shard_map/all_to_all | solution.py:275
  98.0 4.8 %copy-start.6 = (bf16[16,72,384]{2,1,0:T(8,128)(2,1)}, bf16[16,72,384]{2,1,0:T(8,128)(2,1)S(1)}, u32[]{:S(2)}) copy-start(bf16[16,72,384]{2,1,0:T(8,128)(2,1)S(1)} %all-to-all-done) | copy-start | bytes 2654212
  98.0 26.8 %all-to-all-start.3 = ((bf16[16,72,384]{2,1,0:T(8,128)(2,1)}), bf16[16,72,384]{2,1,0:T(8,128)(2,1)S(1)}, u32[]{:S(2)}, u32[]{:S(2)}) async-start(bf16[16,72,384]{2,1,0:T(8,128)(2,1)} %bitcast.22), calls=%async_computation.3 | async-start | bytes 1769472 | tf_op jit(solution)/shard_map/all_to_all | solution.py:275
  124.8 5.4 %copy-start.2 = (bf16[16,72,384]{2,1,0:T(8,128)(2,1)}, bf16[16,72,384]{2,1,0:T(8,128)(2,1)S(1)}, u32[]{:S(2)}) copy-start(bf16[16,72,384]{2,1,0:T(8,128)(2,1)S(1)} %all-to-all-done.3) | copy-start | bytes 2654212
  124.8 27.1 %all-to-all-start.1 = ((bf16[16,72,384]{2,1,0:T(8,128)(2,1)}), bf16[16,72,384]{2,1,0:T(8,128)(2,1)S(1)}, u32[]{:S(2)}, u32[]{:S(2)}) async-start(bf16[16,72,384]{2,1,0:T(8,128)(2,1)} %bitcast.20), calls=%async_computation.1 | async-start | bytes 1769472 | tf_op jit(solution)/shard_map/all_to_all | solution.py:275
  151.9 0.9 copy-start.1
  152.8 4.7 %copy-start.4 = (bf16[2,192,576]{2,1,0:T(8,128)(2,1)S(1)}, bf16[2,192,576]{2,1,0:T(8,128)(2,1)}, u32[]{:S(2)}) copy-start(bf16[2,192,576]{2,1,0:T(8,128)(2,1)} %behind.3) | copy-start | bytes 1327108

commit v2 on v1

--- a/solution.py
+++ b/solution.py
@@ -20,7 +20,6 @@
 CHUNK = X_DEV * GY_DEV
 ROWS = PENCILS * CHUNK
 LANES = EDGE * WIDTH
-BLOCK = 4 * CHUNK
 STATS = 16
 
 bf16 = jnp.bfloat16
@@ -42,6 +41,11 @@
     low = lambda a: np.asarray(a, np.float32).astype(ml_dtypes.bfloat16)
     order = (np.arange(PENCILS)[:, None, None] * X_DEV + np.zeros((1, GY_DEV, 1), int) + np.arange(X_DEV)[None, None, :]).reshape(-1)
     first = np.concatenate([cos.T[order], sin.T[order]], axis=0)
+    pair = np.zeros((2, PENCILS, 2, X_DEV, 2, GBOX))
+    for k in range(2):
+        pair[0, :, k, :, k, :] = cos.T.reshape(PENCILS, X_DEV, GBOX)
+        pair[1, :, k, :, k, :] = sin.T.reshape(PENCILS, X_DEV, GBOX)
+    pair = np.concatenate(list(pair.reshape(2, 2 * GRID, 2 * GBOX)), axis=1)
     core = np.zeros((WIDTH, 512))
     core[:GBOX, :GRID] = cos
     core[GBOX:, :GRID] = -sin
@@ -56,7 +60,7 @@
     back_third = np.zeros((2, 2 * GRID, 256))
     back_third[0, :, :WIDTH] = back
     back_third[1, :, 64:] = back
-    return [low(a) for a in (first, third, second, back_second, back_third)]
+    return [low(a) for a in (first, pair, third, second, back_second, back_third)]
 
 
 def dot(a, b, dims=None):
@@ -67,6 +71,10 @@
 
 def whole(*_):
     return pl.BlockSpec(memory_space=VMEM)
+
+
+def params(mib):
+    return pltpu.CompilerParams(vmem_limit_bytes=mib << 20)
 
 
 def sixth(value):
@@ -95,14 +103,12 @@
         out_shape=(shape, shape),
         in_specs=[whole(), whole()],
         out_specs=(whole(), whole()),
+        compiler_params=params(12),
         name="matrix",
     )(position, first)
 
 
 def stats_kernel(upper_ref, lower_ref, out_ref):
-    def total(a, b):
-        return jnp.sum(a * b)
-
     rows = lax.broadcasted_iota(jnp.int32, (STATS, 128), 0)
     out = jnp.zeros((STATS, 128), f32)
     for j in range(EDGE):
@@ -123,36 +129,47 @@
     return pl.pallas_call(
         stats_kernel,
         out_shape=jax.ShapeDtypeStruct((STATS, 128), f32),
-        in_specs=[whole(), whole()],
+        grid=(1,),
+        in_specs=[whole(), pl.BlockSpec((EDGE, WIDTH, STICKS_DEV), lambda i: (0, 0, 0))],
         out_specs=whole(),
+        compiler_params=params(8),
         name="stats",
     )(upper, lower)
 
 
-def spread_rows(bands, cos_ref, sin_ref, out_ref):
-    plain = jnp.concatenate([part for re, im in bands for part in (re, im)], axis=0)
-    turned = jnp.concatenate([part for re, im in bands for part in (-im, re)], axis=0)
-    for b in range(0, ROWS, BLOCK):
-        rows = pl.ds(b, BLOCK)
-        out_ref[rows, :] = (dot(cos_ref[rows, :], plain, NT) + dot(sin_ref[rows, :], turned, NT)).astype(bf16)
-
-
-def ahead_kernel(bands_ref, cos_ref, sin_ref, out_ref):
-    spread_rows([(bands_ref[b, :GBOX, :], bands_ref[b, GBOX:, :]) for b in range(EDGE)], cos_ref, sin_ref, out_ref)
-
-
-def ahead(bands, cos, sin):
+def spread_rows(bands, map_ref, pair_ref, out_ref):
+    position = map_ref[...]
+    kx = sixth(position)
+    place = GBOX * (position - GY_DEV * kx) + kx
+    select = (lax.broadcasted_iota(jnp.int32, (STICKS_DEV, STICKS_DEV), 0) == place).astype(f32).astype(bf16)
+    both = jnp.concatenate(
+        [part for re, im in bands for part in (re, im)] + [part for re, im in bands for part in (-im, re)], axis=0
+    )
+    placed = dot(select, both, NT).astype(bf16)
+    for p in range(GY_DEV // 2):
+        rows = slice(p * WIDTH, (p + 1) * WIDTH)
+        block = jnp.concatenate([placed[rows, :LANES], placed[rows, LANES:]], axis=0)
+        result = dot(pair_ref[...], block).astype(bf16)
+        out_ref[:, 2 * X_DEV * p : 2 * X_DEV * (p + 1), :] = result.reshape(PENCILS, 2 * X_DEV, LANES)
+
+
+def ahead_kernel(map_ref, bands_ref, pair_ref, out_ref):
+    spread_rows([(bands_ref[b, :GBOX, :], bands_ref[b, GBOX:, :]) for b in range(EDGE)], map_ref, pair_ref, out_ref)
+
+
+def ahead(position, bands, pair):
     return pl.pallas_call(
         ahead_kernel,
-        out_shape=jax.ShapeDtypeStruct((ROWS, LANES), bf16),
+        out_shape=jax.ShapeDtypeStruct((PENCILS, CHUNK, LANES), bf16),
         grid=(1,),
-        in_specs=[pl.BlockSpec((EDGE, WIDTH, STICKS_DEV), lambda i: (1, 0, 0)), whole(), whole()],
+        in_specs=[whole(), pl.BlockSpec((EDGE, WIDTH, STICKS_DEV), lambda i: (1, 0, 0)), whole()],
         out_specs=whole(),
+        compiler_params=params(16),
         name="ahead",
-    )(bands, cos, sin)
-
-
-def edge_kernel(keep_ref, total_ref, bands_ref, upper_ref, cos_ref, sin_ref, out_ref, ortho_ref):
+    )(position, bands, pair)
+
+
+def edge_kernel(keep_ref, total_ref, map_ref, bands_ref, upper_ref, pair_ref, out_ref, ortho_ref):
     bands = []
     for i in range(EDGE):
         u_re = bands_ref[i, :GBOX, :].astype(f32)
@@ -170,33 +187,34 @@
         ortho_ref[i, :GBOX, :] = re
         ortho_ref[i, GBOX:, :] = im
         bands.append((re, im))
-    spread_rows(bands, cos_ref, sin_ref, out_ref)
-
-
-def edge_ahead(keep, total, bands, upper, cos, sin):
+    spread_rows(bands, map_ref, pair_ref, out_ref)
+
+
+def edge_ahead(keep, total, position, bands, upper, pair):
     return pl.pallas_call(
         edge_kernel,
         out_shape=(
-            jax.ShapeDtypeStruct((ROWS, LANES), bf16),
+            jax.ShapeDtypeStruct((PENCILS, CHUNK, LANES), bf16),
             jax.ShapeDtypeStruct((EDGE, WIDTH, STICKS_DEV), bf16),
         ),
         grid=(1,),
         in_specs=[
             pl.BlockSpec(memory_space=pltpu.SMEM),
             whole(),
+            whole(),
             pl.BlockSpec((EDGE, WIDTH, STICKS_DEV), lambda i: (0, 0, 0)),
-            whole(),
             whole(),
             whole(),
         ],
         out_specs=(whole(), whole()),
+        compiler_params=params(16),
         name="edge",
-    )(keep, total, bands, upper, cos, sin)
+    )(keep, total, position, bands, upper, pair)
 
 
 def grid_kernel(rows_ref, potential_ref, third_ref, second_ref, back_second_ref, back_third_ref, out_ref, wide_ref, back_ref):
     for t in range(3):
-        wide_ref[t] = rows_ref[:, 128 * t : 128 * t + 128].astype(f32)
+        wide_ref[t] = rows_ref[:, :, 128 * t : 128 * t + 128].astype(f32).reshape(ROWS, 128)
 
     def plane(x, carry):
         rows = pl.ds(x, GBOX, stride=X_DEV)
@@ -218,7 +236,7 @@
 
     lax.fori_loop(0, X_DEV, plane, 0)
     for t in range(3):
-        out_ref[:, 128 * t : 128 * t + 128] = back_ref[t].astype(bf16)
+        out_ref[:, :, 128 * t : 128 * t + 128] = back_ref[t].reshape(PENCILS, CHUNK, 128).astype(bf16)
 
 
 def on_grid(rows, potential, consts):
@@ -226,10 +244,11 @@
     flops = 2 * EDGE * X_DEV * (96 * 256 * 512 + 384 * 256 * 256 * 2 + 96 * 512 * 256)
     return pl.pallas_call(
         grid_kernel,
-        out_shape=jax.ShapeDtypeStruct((ROWS, LANES), bf16),
+        out_shape=jax.ShapeDtypeStruct((PENCILS, CHUNK, LANES), bf16),
         in_specs=[whole()] * 6,
         out_specs=whole(),
         scratch_shapes=[VMEM((3, ROWS, 128), f32), VMEM((3, ROWS, 128), f32)],
+        compiler_params=params(16),
         cost_estimate=pl.CostEstimate(flops=flops, bytes_accessed=8_000_000, transcendentals=0),
         name="grid",
     )(rows, potential, third, second, back_second, back_third)
@@ -242,7 +261,7 @@
     gy = (position - GY_DEV * kx + GY_DEV * across_ref[0] - GBOX // 2).astype(f32)
     gz = (lax.broadcasted_iota(jnp.int32, (GBOX, STICKS_DEV), 0) - GBOX // 2).astype(f32)
     kinetic = 0.5 * (gx * gx + gy * gy + gz * gz) / float((GBOX // 2) ** 2)
-    rows = rows_ref[...]
+    rows = rows_ref[...].reshape(ROWS, LANES)
     by_cos = dot(rows, cos_ref[...], TN)
     by_sin = dot(rows, sin_ref[...], TN)
     for b in range(EDGE):
@@ -252,57 +271,68 @@
         out_ref[b, GBOX:, :] = (0.5 * (by_cos[im] - by_sin[re]) + kinetic * bands_ref[b, GBOX:, :].astype(f32)).astype(bf16)
 
 
-def behind(position, across, rows, cos, sin, bands, index):
-    return pl.pallas_call(
-        behind_kernel,
-        out_shape=jax.ShapeDtypeStruct((EDGE, WIDTH, STICKS_DEV), bf16),
+def behind(position, across, rows, cos, sin, bands, index, partial=None):
+    block = (EDGE, WIDTH, STICKS_DEV)
+    operands = [position, across, rows, cos, sin, bands]
+    in_specs = [
+        whole(),
+        pl.BlockSpec(memory_space=pltpu.SMEM),
+        whole(),
+        whole(),
+        whole(),
+        pl.BlockSpec(block, lambda i: (index, 0, 0)),
+    ]
+    kernel = behind_kernel
+    if partial is not None:
+        operands.append(partial)
+        in_specs.append(pl.BlockSpec(memory_space=pl.ANY))
+        kernel = lambda *refs: behind_kernel(*refs[:6], refs[7])
+    return pl.pallas_call(
+        kernel,
+        out_shape=jax.ShapeDtypeStruct((2 * EDGE, WIDTH, STICKS_DEV), bf16),
         grid=(1,),
-        in_specs=[
-            whole(),
-            pl.BlockSpec(memory_space=pltpu.SMEM),
-            whole(),
-            whole(),
-            whole(),
-            pl.BlockSpec((EDGE, WIDTH, STICKS_DEV), lambda i: (index, 0, 0)),
-        ],
-        out_specs=whole(),
+        in_specs=in_specs,
+        out_specs=pl.BlockSpec(block, lambda i: (index, 0, 0)),
+        input_output_aliases={} if partial is None else {6: 0},
+        compiler_params=params(16),
         name="behind",
-    )(position, across, rows, cos, sin, bands)
-
-
-def exchange(rows):
-    blocks = rows.reshape(PENCILS, CHUNK, LANES)
-    return lax.all_to_all(blocks, "pencil", split_axis=0, concat_axis=0, tiled=True).reshape(ROWS, LANES)
+    )(*operands)
+
+
+def exchange(blocks):
+    return lax.all_to_all(blocks, "pencil", split_axis=0, concat_axis=0, tiled=True)
 
 
 def total_over_pencil(value):
-    for bit in (2, 4, 8, 1):
-        value = value + lax.ppermute(value, "pencil", [(i, i ^ bit) for i in range(PENCILS)])
+    for bits in ((2, 4, 6), (8, 1, 9)):
+        others = [lax.ppermute(value, "pencil", [(i, i ^ bit) for i in range(PENCILS)]) for bit in bits]
+        value = (value + others[0]) + (others[1] + others[2])
     return value
 
 
-def local(wavefunctions, potential, keep_mask, stick_map):
-    first, *grid_consts = [jnp.asarray(c) for c in constants()]
+def update(wavefunctions, potential, keep_mask, stick_map):
+    first, pair, *grid_consts = [jnp.asarray(c) for c in constants()]
     bands = jnp.transpose(wavefunctions, (0, 2, 1))
     slices = lax.axis_size("cuts")
     upper = lax.ppermute(bands[EDGE:], "cuts", [(i, i + 1) for i in range(slices - 1)])
     position = stick_map.reshape(1, STICKS_DEV)
+    inner_rows = ahead(position, bands, pair)
+    inner_rows = exchange(inner_rows)
+    total = total_over_pencil(stats(upper, bands))
+    edge_rows, ortho = edge_ahead(keep_mask, total, position, bands, upper, pair)
+    edge_rows = exchange(edge_rows)
     cos, sin = build_matrix(position, first)
-    inner_rows = exchange(ahead(bands, cos, sin))
-    total = total_over_pencil(stats(upper, bands[:EDGE]))
-    edge_rows, ortho = edge_ahead(keep_mask, total, bands, upper, cos, sin)
-    edge_rows = exchange(edge_rows)
     inner_back = exchange(on_grid(inner_rows, potential, grid_consts))
     edge_back = exchange(on_grid(edge_rows, potential, grid_consts))
     across = lax.axis_index("pencil").reshape(1).astype(jnp.int32)
     inner_out = behind(position, across, inner_back, cos, sin, bands, 1)
-    edge_out = behind(position, across, edge_back, cos, sin, ortho, 0)
-    return jnp.transpose(jnp.concatenate([edge_out, inner_out], axis=0), (0, 2, 1))
+    out = behind(position, across, edge_back, cos, sin, ortho, 0, inner_out)
+    return jnp.transpose(out, (0, 2, 1))
 
 
 def solution(mesh):
     return jax.shard_map(
-        local,
+        update,
         mesh=mesh,
         in_specs=(
             P("cuts", "pencil", None),

time: 160 us -> 151 us (0.944); the launches traced: 160 us -> 149 us
  Pallas kernels: 60.5 us -> 41.3 us
  local copies, waits for them, and re-layouts: 3.87 us -> 19.5 us
  other arithmetic: 3.41 us -> 0.01 us
  starting transfers between devices: 47.4 us -> 44.8 us
    unnamed x14 -> x50, local copies, waits for them, and re-layouts: 1.72 us -> 18.8 us
    pallas_call x6, Pallas kernels: 54.8 us -> 39.5 us  [the longest x2 29.1 us: on_grid(): pl.pallas_call(grid_kernel, out_shape=jax.ShapeDtypeStruct((PENCILS, CHUN...]
    all_to_all x4, starting transfers between devices: 31.1 us -> 27.7 us  [exchange(): lax.all_to_all(blocks, 'pencil', split_axis=0, concat_axis=0, tiled=True)]
    pallas_call x1, Pallas kernels: 3.38 us -> 1.18 us  [build_matrix(): pl.pallas_call(matrix_kernel, out_shape=(shape, shape), in_specs=[whole()...]
    transpose x1 -> x0, other arithmetic: 2.11 us -> none  [local(): jnp.transpose(jnp.concatenate([edge_out, inner_out], axis=0), (0, 2, 1))]
    all_to_all x4, waiting for transfers between devices: 26.2 us -> 24.1 us  [exchange(): lax.all_to_all(blocks, 'pencil', split_axis=0, concat_axis=0, tiled=True)]
    pallas_call x1, Pallas kernels: 2.37 us -> 0.61 us  [stats(): pl.pallas_call(stats_kernel, out_shape=jax.ShapeDtypeStruct((STATS, 128),...]
    ppermute x4 -> x6, waiting for transfers between devices: 9.31 us -> 9.99 us  [total_over_pencil(): lax.ppermute(value, 'pencil', [(i, i ^ bit) for i in range(PENCILS)])]
  transfers between devices with their start and end apart: 9 -> 11, of which waited for: 8 -> 8; matrix products, arithmetic and copies ran while one was open for 1% -> 0% of each run, Pallas kernels for 30% -> 24%
where the time goes in v2:
time: 151 us; the launch traced here: 149 us
  starting transfers between devices  44.8 us (30%)
  waiting for transfers between devices  42.9 us (28%)
  Pallas kernels  41.3 us (27%)
  local copies, waits for them, and re-layouts  19.5 us (13%)
    pallas_call x2, Pallas kernels, on_grid(): pl.pallas_call(grid_kernel, out_shape=jax.ShapeDtypeStruct((PENCILS, CHUN...  29.1 us
    all_to_all x4, starting transfers between devices, exchange(): lax.all_to_all(blocks, 'pencil', split_axis=0, concat_axis=0, tiled=True)  27.7 us
    all_to_all x4, waiting for transfers between devices, exchange(): lax.all_to_all(blocks, 'pencil', split_axis=0, concat_axis=0, tiled=True)  24.1 us
    unnamed x50, local copies, waits for them, and re-layouts  18.8 us
    ppermute x6, starting transfers between devices, total_over_pencil(): lax.ppermute(value, 'pencil', [(i, i ^ bit) for i in range(PENCILS)])  15 us
    ppermute x6, waiting for transfers between devices, total_over_pencil(): lax.ppermute(value, 'pencil', [(i, i ^ bit) for i in range(PENCILS)])  9.99 us
    ppermute x1, waiting for transfers between devices, update(): lax.ppermute(bands[EDGE:], 'cuts', [(i, i + 1) for i in range(slices - 1)])  8.81 us
    pallas_call x2, Pallas kernels, behind(): pl.pallas_call(kernel, out_shape=jax.ShapeDtypeStruct((2 * EDGE, WIDTH, S...  4.9 us
  transfers between devices with their start and end apart: 11, of which 8 were waited for; matrix products, arithmetic and copies ran while one was open for 0% of the time, Pallas kernels for 24%

profile of v2, /device:TPU:10, one launch (start us, length us, event | category | flops | bytes accessed | tf_op | source)
XLA Modules:
  0.0 148.8 jit_solution(13849305694834152947)
XLA Ops:
  0.7 1.2 copy-done
  2.9 2.8 %ahead.1 = bf16[16,72,384]{2,1,0:T(8,128)(2,1)} custom-call(s32[1,576]{1,0:T(1,128)S(1)} %reshape.6.map_ref.refs_0_, bf16[4,192,576]{2,1,0:T(8,128)(2,1)S(1)} %bitcast.3, bf16[384,384]{1,0:T(8,128)(2,1)S(1)} %copy-done.6), custom_call_target="tpu_custom_call" | custom-call | tf_op jit(solution)/shard_map/ahead/pallas_call | solution.py:161
  5.6 10.1 %all-to-all-start.2 = ((bf16[16,72,384]{2,1,0:T(8,128)(2,1)}), bf16[16,72,384]{2,1,0:T(8,128)(2,1)S(1)}, u32[]{:S(2)}, u32[]{:S(2)}) async-start(bf16[16,72,384]{2,1,0:T(8,128)(2,1)} %ahead.1), calls=%async_computation.2 | async-start | bytes 1769472 | tf_op jit(solution)/shard_map/all_to_all | solution.py:303
  15.9 2.1 %collective-permute-start = (bf16[2,192,576]{2,1,0:T(8,128)(2,1)S(1)}, bf16[2,192,576]{2,1,0:T(8,128)(2,1)S(1)}, u32[]{:S(2)}, u32[]{:S(2)}) collective-permute-start(bf16[2,192,576]{2,1,0:T(8,128)(2,1)S(1)} %slice.4), channel_id=1, source_target_pairs={{0,16},{16,32},{32,48},{48,64},{64,80},{80,96},{96,112},{112,128},... | collective-permute-start | bytes 1327112 | tf_op jit(solution)/shard_map/ppermute | solution.py:317
  17.9 8.8 %collective-permute-done.upper_ref = bf16[2,192,576]{2,1,0:T(8,128)(2,1)S(1)} collective-permute-done((bf16[2,192,576]{2,1,0:T(8,128)(2,1)S(1)}, bf16[2,192,576]{2,1,0:T(8,128)(2,1)S(1)}, u32[]{:S(2)}, u32[]{:S(2)}) %collective-permute-start) | collective-permute-done | bytes 442400 | tf_op jit(solution)/shard_map/ppermute | solution.py:317
  27.4 5.3 %collective-permute-start.3 = (f32[16,128]{1,0:T(8,128)S(1)}, f32[16,128]{1,0:T(8,128)S(1)}, u32[]{:S(2)}, u32[]{:S(2)}) collective-permute-start(f32[16,128]{1,0:T(8,128)S(1)} %stats.1), channel_id=1, source_target_pairs={{0,6},{1,7},{2,4},{3,5},{4,2},{5,3},{6,0},{7,1},{8,14},{9,15},{10,... | collective-permute-start | bytes 24584 | tf_op jit(solution)/shard_map/ppermute | solution.py:308
  33.4 5.5 %collective-permute-done.3 = f32[16,128]{1,0:T(8,128)S(1)} collective-permute-done((f32[16,128]{1,0:T(8,128)S(1)}, f32[16,128]{1,0:T(8,128)S(1)}, u32[]{:S(2)}, u32[]{:S(2)}) %collective-permute-start.3) | collective-permute-done | bytes 8224 | tf_op jit(solution)/shard_map/ppermute | solution.py:308
  38.9 5.8 %collective-permute-start.6 = (f32[16,128]{1,0:T(8,128)S(1)}, f32[16,128]{1,0:T(8,128)S(1)}, u32[]{:S(2)}, u32[]{:S(2)}) collective-permute-start(f32[16,128]{1,0:T(8,128)S(1)} %add_add_fusion.1), channel_id=1, source_target_pairs={{0,9},{1,8},{2,11},{3,10},{4,13},{5,12},{6,15},{7,14},{8,1},{9,0},... | collective-permute-start | bytes 24584 | tf_op jit(solution)/shard_map/ppermute | solution.py:308
  44.8 3.1 %collective-permute-start.4 = (f32[16,128]{1,0:T(8,128)S(1)}, f32[16,128]{1,0:T(8,128)S(1)}, u32[]{:S(2)}, u32[]{:S(2)}) collective-permute-start(f32[16,128]{1,0:T(8,128)S(1)} %add_add_fusion.1), channel_id=1, source_target_pairs={{0,8},{1,9},{2,10},{3,11},{4,12},{5,13},{6,14},{7,15},{8,0},{9,1},... | collective-permute-start | bytes 24584 | tf_op jit(solution)/shard_map/ppermute | solution.py:308
  47.9 1.1 collective-permute-done.6
  49.9 2.5 %collective-permute-done.4 = f32[16,128]{1,0:T(8,128)S(1)} collective-permute-done((f32[16,128]{1,0:T(8,128)S(1)}, f32[16,128]{1,0:T(8,128)S(1)}, u32[]{:S(2)}, u32[]{:S(2)}) %collective-permute-start.4) | collective-permute-done | bytes 8224 | tf_op jit(solution)/shard_map/ppermute | solution.py:308
  52.4 2.7 %edge.1 = (bf16[16,72,384]{2,1,0:T(8,128)(2,1)S(1)}, bf16[2,192,576]{2,1,0:T(8,128)(2,1)S(1)}) custom-call(s32[1,2,2]{2,1,0:T(2,128)S(1)} %copy-done.16, f32[16,128]{1,0:T(8,128)S(1)} %add_add_fusion.total_ref, s32[1,576]{1,0:T(1,128)S(1)} %reshape.6.map_ref.refs_0_, bf16[4,192,576]{2,1,0:T(8,128)(2,1)S(1)} %bitcast.6, ...), custom_call_target="tpu_custom_call" | custom-call | tf_op jit(solution)/shard_map/edge/pallas_call | solution.py:194
  56.8 7.2 %all-to-all-start = ((bf16[16,72,384]{2,1,0:T(8,128)(2,1)}), bf16[16,72,384]{2,1,0:T(8,128)(2,1)S(1)}, u32[]{:S(2)}, u32[]{:S(2)}) async-start(bf16[16,72,384]{2,1,0:T(8,128)(2,1)} %copy-done.11), calls=%async_computation | async-start | bytes 1769472 | tf_op jit(solution)/shard_map/all_to_all | solution.py:303
  64.0 1.7 %copy-done.17 = f32[12,192,192]{2,1,0:T(8,128)S(1)} copy-done((f32[12,192,192]{2,1,0:T(8,128)S(1)}, f32[12,192,192]{2,1,0:T(8,128)}, u32[]{:S(2)}) %copy-start.17) | copy-done | bytes 1769496
  65.7 1.0 copy-done.20
  67.6 14.5 %grid.3 = bf16[16,72,384]{2,1,0:T(8,128)(2,1)S(1)} custom-call(bf16[16,72,384]{2,1,0:T(8,128)(2,1)S(1)} %all-to-all-done.2.rows_ref, f32[12,192,192]{2,1,0:T(8,128)S(1)} %copy-done.17, bf16[2,256,512]{2,1,0:T(8,128)(2,1)S(1)} %copy-done.19, bf16[384,192]{1,0:T(8,128)(2,1)S(1)} %copy-done.22, bf16[192,384]{1,0:T(8,128)(2,1)S(1)} %copy-done.23, ...), custom_call_target="tpu_custom_call" | custom-call | flops 3623878656 | bytes 8000000 | tf_op jit(solution)/shard_map/grid/pallas_call | solution.py:245
  83.1 4.4 %all-to-all-done.rows_ref = bf16[16,72,384]{2,1,0:T(8,128)(2,1)S(1)} async-done(((bf16[16,72,384]{2,1,0:T(8,128)(2,1)}), bf16[16,72,384]{2,1,0:T(8,128)(2,1)S(1)}, u32[]{:S(2)}, u32[]{:S(2)}) %all-to-all-start) | async-done | bytes 884768 | tf_op jit(solution)/shard_map/all_to_all | solution.py:303
  88.4 5.2 %all-to-all-start.3 = ((bf16[16,72,384]{2,1,0:T(8,128)(2,1)}), bf16[16,72,384]{2,1,0:T(8,128)(2,1)S(1)}, u32[]{:S(2)}, u32[]{:S(2)}) async-start(bf16[16,72,384]{2,1,0:T(8,128)(2,1)} %copy-done.12), calls=%async_computation.3 | async-start | bytes 1769472 | tf_op jit(solution)/shard_map/all_to_all | solution.py:303
  93.7 1.2 copy-done.10
  94.8 1.7 %copy-done.18 = f32[12,192,192]{2,1,0:T(8,128)S(1)} copy-done((f32[12,192,192]{2,1,0:T(8,128)S(1)}, f32[12,192,192]{2,1,0:T(8,128)}, u32[]{:S(2)}) %copy-start.18) | copy-done | bytes 1769496
  96.5 14.5 %grid.2 = bf16[16,72,384]{2,1,0:T(8,128)(2,1)S(1)} custom-call(bf16[16,72,384]{2,1,0:T(8,128)(2,1)S(1)} %copy-done.10, f32[12,192,192]{2,1,0:T(8,128)S(1)} %copy-done.18, bf16[2,256,512]{2,1,0:T(8,128)(2,1)S(1)} %copy-done.19, bf16[384,192]{1,0:T(8,128)(2,1)S(1)} %copy-done.22, bf16[192,384]{1,0:T(8,128)(2,1)S(1)} %copy-done.24, ...), custom_call_target="tpu_custom_call" | custom-call | flops 3623878656 | bytes 8000000 | tf_op jit(solution)/shard_map/grid/pallas_call | solution.py:245
  112.0 4.4 %all-to-all-done.3.rows_ref = bf16[16,72,384]{2,1,0:T(8,128)(2,1)S(1)} async-done(((bf16[16,72,384]{2,1,0:T(8,128)(2,1)}), bf16[16,72,384]{2,1,0:T(8,128)(2,1)S(1)}, u32[]{:S(2)}, u32[]{:S(2)}) %all-to-all-start.3) | async-done | bytes 884768 | tf_op jit(solution)/shard_map/all_to_all | solution.py:303
  116.4 5.2 %all-to-all-start.1 = ((bf16[16,72,384]{2,1,0:T(8,128)(2,1)}), bf16[16,72,384]{2,1,0:T(8,128)(2,1)S(1)}, u32[]{:S(2)}, u32[]{:S(2)}) async-start(bf16[16,72,384]{2,1,0:T(8,128)(2,1)} %copy-done.8), calls=%async_computation.1 | async-start | bytes 1769472 | tf_op jit(solution)/shard_map/all_to_all | solution.py:303
  121.6 1.1 copy-done.13
  122.7 1.2 matrix.1
  123.9 1.2 copy-done.5
  125.1 2.5 %behind.2.refs_6_ = bf16[4,192,576]{2,1,0:T(8,128)(2,1)} custom-call(s32[1,576]{1,0:T(1,128)S(1)} %reshape.6.map_ref.refs_0_, s32[1]{0:T(128)} %bitcast.across_ref.refs_1_, bf16[16,72,384]{2,1,0:T(8,128)(2,1)S(1)} %copy-done.5, bf16[1152,576]{1,0:T(8,128)(2,1)S(1)} %get-tuple-element.10.cos_ref.refs_3_, ...), custom_call_target="tpu_custom_call" | custom-call | tf_op jit(solution)/shard_map/behind/pallas_call | solution.py:290
  127.5 1.1 copy-done.2
  128.6 15.3 %all-to-all-done.1.refs_2_ = bf16[16,72,384]{2,1,0:T(8,128)(2,1)S(1)} async-done(((bf16[16,72,384]{2,1,0:T(8,128)(2,1)}), bf16[16,72,384]{2,1,0:T(8,128)(2,1)S(1)}, u32[]{:S(2)}, u32[]{:S(2)}) %all-to-all-start.1) | async-done | bytes 884768 | tf_op jit(solution)/shard_map/all_to_all | solution.py:303
  143.9 1.4 copy-done.3
  145.3 1.0 copy-done.15
  146.3 2.5 %behind.3 = bf16[4,192,576]{2,1,0:T(8,128)(2,1)} custom-call(s32[1,576]{1,0:T(1,128)S(1)} %reshape.6.map_ref.refs_0_, s32[1]{0:T(128)} %bitcast.across_ref.refs_1_, bf16[16,72,384]{2,1,0:T(8,128)(2,1)S(1)} %all-to-all-done.1.refs_2_, bf16[1152,576]{1,0:T(8,128)(2,1)S(1)} %get-tuple-element.10.cos_ref.refs_3_, ...), custom_call_target="tpu_custom_call", output_to_operand_aliasing={{}: (6, {})} | custom-call | tf_op jit(solution)/shard_map/behind/pallas_call | solution.py:290
  (52 shorter events, 9.4 us)
Async XLA Ops:
  0.7 1.2 copy-start
  1.9 1.0 copy-start.6
  2.9 12.9 %copy-start.1 = (bf16[4,576,192]{1,2,0:T(8,128)(2,1)S(1)}, bf16[4,576,192]{1,2,0:T(8,128)(2,1)}, u32[]{:S(2)}) copy-start(bf16[4,576,192]{1,2,0:T(8,128)(2,1)} %param.10) | copy-start | bytes 2654212
  5.6 51.1 %all-to-all-start.2 = ((bf16[16,72,384]{2,1,0:T(8,128)(2,1)}), bf16[16,72,384]{2,1,0:T(8,128)(2,1)S(1)}, u32[]{:S(2)}, u32[]{:S(2)}) async-start(bf16[16,72,384]{2,1,0:T(8,128)(2,1)} %ahead.1), calls=%async_computation.2 | async-start | bytes 1769472 | tf_op jit(solution)/shard_map/all_to_all | solution.py:303
  15.8 36.6 %copy-start.7 = (bf16[384,384]{1,0:T(8,128)(2,1)S(1)}, bf16[384,384]{1,0:T(8,128)(2,1)}, u32[]{:S(2)}) copy-start(bf16[384,384]{1,0:T(8,128)(2,1)} %constant.17.clone.pair_ref) | copy-start | bytes 884740
  15.8 36.6 %copy-start.16 = (s32[1,2,2]{2,1,0:T(2,128)S(1)}, s32[1,2,2]{2,1,0:T(2,128)}, u32[]{:S(2)}) copy-start(s32[1,2,2]{2,1,0:T(2,128)} %keep_ref.1) | copy-start | bytes 52
  15.9 10.9 %collective-permute-start = (bf16[2,192,576]{2,1,0:T(8,128)(2,1)S(1)}, bf16[2,192,576]{2,1,0:T(8,128)(2,1)S(1)}, u32[]{:S(2)}, u32[]{:S(2)}) collective-permute-start(bf16[2,192,576]{2,1,0:T(8,128)(2,1)S(1)} %slice.4), channel_id=1, source_target_pairs={{0,16},{16,32},{32,48},{48,64},{64,80},{80,96},{96,112},{112,128},... | collective-permute-start | bytes 1327112 | tf_op jit(solution)/shard_map/ppermute | solution.py:317
  27.4 11.5 %collective-permute-start.3 = (f32[16,128]{1,0:T(8,128)S(1)}, f32[16,128]{1,0:T(8,128)S(1)}, u32[]{:S(2)}, u32[]{:S(2)}) collective-permute-start(f32[16,128]{1,0:T(8,128)S(1)} %stats.1), channel_id=1, source_target_pairs={{0,6},{1,7},{2,4},{3,5},{4,2},{5,3},{6,0},{7,1},{8,14},{9,15},{10,... | collective-permute-start | bytes 24584 | tf_op jit(solution)/shard_map/ppermute | solution.py:308
  32.7 6.2 %collective-permute-start.2 = (f32[16,128]{1,0:T(8,128)S(1)}, f32[16,128]{1,0:T(8,128)S(1)}, u32[]{:S(2)}, u32[]{:S(2)}) collective-permute-start(f32[16,128]{1,0:T(8,128)S(1)} %stats.1), channel_id=1, source_target_pairs={{0,4},{1,5},{2,6},{3,7},{4,0},{5,1},{6,2},{7,3},{8,12},{9,13},{10,... | collective-permute-start | bytes 24584 | tf_op jit(solution)/shard_map/ppermute | solution.py:308
  32.7 6.2 %collective-permute-start.1 = (f32[16,128]{1,0:T(8,128)S(1)}, f32[16,128]{1,0:T(8,128)S(1)}, u32[]{:S(2)}, u32[]{:S(2)}) collective-permute-start(f32[16,128]{1,0:T(8,128)S(1)} %stats.1), channel_id=1, source_target_pairs={{0,2},{1,3},{2,0},{3,1},{4,6},{5,7},{6,4},{7,5},{8,10},{9,11},{10,... | collective-permute-start | bytes 24584 | tf_op jit(solution)/shard_map/ppermute | solution.py:308
  38.9 10.0 %collective-permute-start.6 = (f32[16,128]{1,0:T(8,128)S(1)}, f32[16,128]{1,0:T(8,128)S(1)}, u32[]{:S(2)}, u32[]{:S(2)}) collective-permute-start(f32[16,128]{1,0:T(8,128)S(1)} %add_add_fusion.1), channel_id=1, source_target_pairs={{0,9},{1,8},{2,11},{3,10},{4,13},{5,12},{6,15},{7,14},{8,1},{9,0},... | collective-permute-start | bytes 24584 | tf_op jit(solution)/shard_map/ppermute | solution.py:308
  44.7 5.2 %collective-permute-start.5 = (f32[16,128]{1,0:T(8,128)S(1)}, f32[16,128]{1,0:T(8,128)S(1)}, u32[]{:S(2)}, u32[]{:S(2)}) collective-permute-start(f32[16,128]{1,0:T(8,128)S(1)} %add_add_fusion.1), channel_id=1, source_target_pairs={{0,1},{1,0},{2,3},{3,2},{4,5},{5,4},{6,7},{7,6},{8,9},{9,8},{10,11... | collective-permute-start | bytes 24584 | tf_op jit(solution)/shard_map/ppermute | solution.py:308
  44.8 7.6 %collective-permute-start.4 = (f32[16,128]{1,0:T(8,128)S(1)}, f32[16,128]{1,0:T(8,128)S(1)}, u32[]{:S(2)}, u32[]{:S(2)}) collective-permute-start(f32[16,128]{1,0:T(8,128)S(1)} %add_add_fusion.1), channel_id=1, source_target_pairs={{0,8},{1,9},{2,10},{3,11},{4,12},{5,13},{6,14},{7,15},{8,0},{9,1},... | collective-permute-start | bytes 24584 | tf_op jit(solution)/shard_map/ppermute | solution.py:308
  52.4 11.6 %copy-start.19 = (bf16[2,256,512]{2,1,0:T(8,128)(2,1)S(1)}, bf16[2,256,512]{2,1,0:T(8,128)(2,1)}, u32[]{:S(2)}) copy-start(bf16[2,256,512]{2,1,0:T(8,128)(2,1)} %constant.18.clone.third_ref) | copy-start | bytes 1572868
  52.4 11.6 %copy-start.22 = (bf16[384,192]{1,0:T(8,128)(2,1)S(1)}, bf16[384,192]{1,0:T(8,128)(2,1)}, u32[]{:S(2)}) copy-start(bf16[384,192]{1,0:T(8,128)(2,1)} %constant.19.clone.second_ref) | copy-start | bytes 442372
  56.8 30.7 %all-to-all-start = ((bf16[16,72,384]{2,1,0:T(8,128)(2,1)}), bf16[16,72,384]{2,1,0:T(8,128)(2,1)S(1)}, u32[]{:S(2)}, u32[]{:S(2)}) async-start(bf16[16,72,384]{2,1,0:T(8,128)(2,1)} %copy-done.11), calls=%async_computation | async-start | bytes 1769472 | tf_op jit(solution)/shard_map/all_to_all | solution.py:303
  64.0 1.7 %copy-start.17 = (f32[12,192,192]{2,1,0:T(8,128)S(1)}, f32[12,192,192]{2,1,0:T(8,128)}, u32[]{:S(2)}) copy-start(f32[12,192,192]{2,1,0:T(8,128)} %potential_ref.3) | copy-start | bytes 5308420
  65.7 1.0 copy-start.20
  82.2 0.9 copy-start.12
  83.1 10.5 %copy-start.21 = (bf16[2,384,256]{2,1,0:T(8,128)(2,1)S(1)}, bf16[2,384,256]{2,1,0:T(8,128)(2,1)}, u32[]{:S(2)}) copy-start(bf16[2,384,256]{2,1,0:T(8,128)(2,1)} %constant.21.clone.back_third_ref) | copy-start | bytes 1179652
  83.1 10.6 %copy-start.24 = (bf16[192,384]{1,0:T(8,128)(2,1)S(1)}, bf16[192,384]{1,0:T(8,128)(2,1)}, u32[]{:S(2)}) copy-start(bf16[192,384]{1,0:T(8,128)(2,1)} %constant.20.clone.back_second_ref) | copy-start | bytes 442372
  88.4 28.0 %all-to-all-start.3 = ((bf16[16,72,384]{2,1,0:T(8,128)(2,1)}), bf16[16,72,384]{2,1,0:T(8,128)(2,1)S(1)}, u32[]{:S(2)}, u32[]{:S(2)}) async-start(bf16[16,72,384]{2,1,0:T(8,128)(2,1)} %copy-done.12), calls=%async_computation.3 | async-start | bytes 1769472 | tf_op jit(solution)/shard_map/all_to_all | solution.py:303
  93.7 1.2 copy-start.10
  94.8 1.7 %copy-start.18 = (f32[12,192,192]{2,1,0:T(8,128)S(1)}, f32[12,192,192]{2,1,0:T(8,128)}, u32[]{:S(2)}) copy-start(f32[12,192,192]{2,1,0:T(8,128)} %potential_ref.3) | copy-start | bytes 5308420
  111.1 0.9 copy-start.8
  116.4 5.2 %copy-start.4 = (bf16[16,72,384]{2,1,0:T(8,128)(2,1)}, bf16[16,72,384]{2,1,0:T(8,128)(2,1)S(1)}, u32[]{:S(2)}) copy-start(bf16[16,72,384]{2,1,0:T(8,128)(2,1)S(1)} %all-to-all-done.3.rows_ref) | copy-start | bytes 2654212
  116.4 27.5 %all-to-all-start.1 = ((bf16[16,72,384]{2,1,0:T(8,128)(2,1)}), bf16[16,72,384]{2,1,0:T(8,128)(2,1)S(1)}, u32[]{:S(2)}, u32[]{:S(2)}) async-start(bf16[16,72,384]{2,1,0:T(8,128)(2,1)} %copy-done.8), calls=%async_computation.1 | async-start | bytes 1769472 | tf_op jit(solution)/shard_map/all_to_all | solution.py:303
  121.6 1.1 copy-start.13
  123.9 1.2 copy-start.5
  127.5 1.1 copy-start.2
  143.9 1.4 copy-start.3
  145.3 1.0 copy-start.15
  (4 other events, 3.5 us)

commit v3 on v2

--- a/solution.py
+++ b/solution.py
@@ -20,7 +20,6 @@
 CHUNK = X_DEV * GY_DEV
 ROWS = PENCILS * CHUNK
 LANES = EDGE * WIDTH
-STATS = 16
 
 bf16 = jnp.bfloat16
 f32 = jnp.float32
@@ -108,36 +107,55 @@
     )(position, first)
 
 
-def stats_kernel(upper_ref, lower_ref, out_ref):
-    rows = lax.broadcasted_iota(jnp.int32, (STATS, 128), 0)
-    out = jnp.zeros((STATS, 128), f32)
+def start_copy(source, target, sem):
+    copy = pltpu.make_async_copy(source, target, sem)
+    copy.start()
+    return copy
+
+
+def stats_kernel(upper_ref, lower_ref, _, out_ref, block_ref, sem):
+    terms = []
     for j in range(EDGE):
         p_re = upper_ref[j, :GBOX, :].astype(f32)
         p_im = upper_ref[j, GBOX:, :].astype(f32)
         for i in range(EDGE):
             u_re = lower_ref[i, :GBOX, :].astype(f32)
             u_im = lower_ref[i, GBOX:, :].astype(f32)
-            real = jnp.sum(p_re * u_re + p_im * u_im)
-            imag = jnp.sum(p_re * u_im - p_im * u_re)
-            out = jnp.where(rows == 2 * j + i, real, out)
-            out = jnp.where(rows == 4 + 2 * j + i, imag, out)
-        out = jnp.where(rows == 8 + j, jnp.sum(p_re * p_re + p_im * p_im), out)
-    out_ref[...] = out
-
-
-def stats(upper, lower):
+            terms.append((2 * j + i, jnp.sum(p_re * u_re + p_im * u_im)))
+            terms.append((4 + 2 * j + i, jnp.sum(p_re * u_im - p_im * u_re)))
+        terms.append((8 + j, jnp.sum(p_re * p_re + p_im * p_im)))
+    lane = lax.broadcasted_iota(jnp.int32, (8, LANES), 1)
+    row = lax.broadcasted_iota(jnp.int32, (8, LANES), 0)
+    value = jnp.zeros((8, LANES), f32)
+    for k, term in terms:
+        value = jnp.where(lane == k, term, value)
+    high = value.astype(bf16).astype(f32)
+    middle = (value - high).astype(bf16).astype(f32)
+    rest = value - high - middle
+    packed = jnp.where(row == 0, high, jnp.where(row == 1, middle, jnp.where(row == 2, rest, 0.0))).astype(bf16)
+    block_ref[...] = jnp.broadcast_to(packed[None], (PENCILS, 8, LANES))
+    start_copy(block_ref, out_ref.at[:, CHUNK:, :], sem).wait()
+
+
+def stats(upper, bands, payload):
     return pl.pallas_call(
         stats_kernel,
-        out_shape=jax.ShapeDtypeStruct((STATS, 128), f32),
+        out_shape=jax.ShapeDtypeStruct((PENCILS, CHUNK + 8, LANES), bf16),
         grid=(1,),
-        in_specs=[whole(), pl.BlockSpec((EDGE, WIDTH, STICKS_DEV), lambda i: (0, 0, 0))],
-        out_specs=whole(),
+        in_specs=[
+            whole(),
+            pl.BlockSpec((EDGE, WIDTH, STICKS_DEV), lambda i: (0, 0, 0)),
+            pl.BlockSpec(memory_space=pltpu.HBM),
+        ],
+        out_specs=pl.BlockSpec(memory_space=pltpu.HBM),
+        scratch_shapes=[VMEM((PENCILS, 8, LANES), bf16), pltpu.SemaphoreType.DMA(())],
+        input_output_aliases={2: 0},
         compiler_params=params(8),
         name="stats",
-    )(upper, lower)
-
-
-def spread_rows(bands, map_ref, pair_ref, out_ref):
+    )(upper, bands, payload)
+
+
+def spread_rows(bands, map_ref, pair_ref, out_ref, block_ref, sems):
     position = map_ref[...]
     kx = sixth(position)
     place = GBOX * (position - GY_DEV * kx) + kx
@@ -146,39 +164,56 @@
         [part for re, im in bands for part in (re, im)] + [part for re, im in bands for part in (-im, re)], axis=0
     )
     placed = dot(select, both, NT).astype(bf16)
+    copies = []
     for p in range(GY_DEV // 2):
         rows = slice(p * WIDTH, (p + 1) * WIDTH)
         block = jnp.concatenate([placed[rows, :LANES], placed[rows, LANES:]], axis=0)
         result = dot(pair_ref[...], block).astype(bf16)
-        out_ref[:, 2 * X_DEV * p : 2 * X_DEV * (p + 1), :] = result.reshape(PENCILS, 2 * X_DEV, LANES)
-
-
-def ahead_kernel(map_ref, bands_ref, pair_ref, out_ref):
-    spread_rows([(bands_ref[b, :GBOX, :], bands_ref[b, GBOX:, :]) for b in range(EDGE)], map_ref, pair_ref, out_ref)
+        block_ref[p] = result.reshape(PENCILS, 2 * X_DEV, LANES)
+        copies.append(start_copy(block_ref.at[p], out_ref.at[:, 2 * X_DEV * p : 2 * X_DEV * (p + 1), :], sems.at[p]))
+    for copy in copies:
+        copy.wait()
+
+
+def spread_scratch():
+    return [VMEM((GY_DEV // 2, PENCILS, 2 * X_DEV, LANES), bf16), pltpu.SemaphoreType.DMA((GY_DEV // 2,))]
+
+
+def ahead_kernel(map_ref, bands_ref, pair_ref, out_ref, *rest):
+    block_ref, sems = rest[-2:]
+    bands = [(bands_ref[b, :GBOX, :], bands_ref[b, GBOX:, :]) for b in range(EDGE)]
+    spread_rows(bands, map_ref, pair_ref, out_ref, block_ref, sems)
+
+
+HBM = pl.BlockSpec(memory_space=pltpu.HBM)
+ROWS_SHAPE = jax.ShapeDtypeStruct((PENCILS, CHUNK, LANES), bf16)
+BANDS_SHAPE = jax.ShapeDtypeStruct((EDGE, WIDTH, STICKS_DEV), bf16)
 
 
 def ahead(position, bands, pair):
     return pl.pallas_call(
         ahead_kernel,
-        out_shape=jax.ShapeDtypeStruct((PENCILS, CHUNK, LANES), bf16),
+        out_shape=(jax.ShapeDtypeStruct((PENCILS, CHUNK + 8, LANES), bf16), BANDS_SHAPE, ROWS_SHAPE, ROWS_SHAPE, ROWS_SHAPE),
         grid=(1,),
         in_specs=[whole(), pl.BlockSpec((EDGE, WIDTH, STICKS_DEV), lambda i: (1, 0, 0)), whole()],
-        out_specs=whole(),
-        compiler_params=params(16),
+        out_specs=(HBM,) * 5,
+        scratch_shapes=spread_scratch(),
+        compiler_params=params(60),
         name="ahead",
     )(position, bands, pair)
 
 
-def edge_kernel(keep_ref, total_ref, map_ref, bands_ref, upper_ref, pair_ref, out_ref, ortho_ref):
+def edge_kernel(keep_ref, sums_ref, map_ref, bands_ref, upper_ref, pair_ref, _, __, out_ref, ortho_out_ref, block_ref, sems, ortho_ref, ortho_sem):
+    total = jnp.sum(jnp.sum(sums_ref[...].astype(f32), axis=0), axis=0, keepdims=True)
     bands = []
     for i in range(EDGE):
         u_re = bands_ref[i, :GBOX, :].astype(f32)
         u_im = bands_ref[i, GBOX:, :].astype(f32)
         for j in range(EDGE):
             keep = keep_ref[0, i, j].astype(f32)
-            divisor = total_ref[8 + j : 9 + j, 0:1] + 1e-05
-            w_re = keep * total_ref[2 * j + i : 2 * j + i + 1, 0:1] / divisor
-            w_im = keep * total_ref[4 + 2 * j + i : 5 + 2 * j + i, 0:1] / divisor
+            divisor = total[:, 8 + j : 9 + j] + 1e-05
+            w_re = keep * total[:, 2 * j + i : 2 * j + i + 1] / divisor
+            w_im = keep * total[:, 4 + 2 * j + i : 5 + 2 * j + i] / divisor
             p_re = upper_ref[j, :GBOX, :].astype(f32)
             p_im = upper_ref[j, GBOX:, :].astype(f32)
             u_re = u_re - (w_re * p_re - w_im * p_im)
@@ -187,71 +222,126 @@
         ortho_ref[i, :GBOX, :] = re
         ortho_ref[i, GBOX:, :] = im
         bands.append((re, im))
-    spread_rows(bands, map_ref, pair_ref, out_ref)
-
-
-def edge_ahead(keep, total, position, bands, upper, pair):
+    copy = start_copy(ortho_ref, ortho_out_ref, ortho_sem)
+    spread_rows(bands, map_ref, pair_ref, out_ref, block_ref, sems)
+    copy.wait()
+
+
+def edge_ahead(keep, sums, position, bands, upper, pair, rows_buffer, ortho_buffer):
     return pl.pallas_call(
         edge_kernel,
-        out_shape=(
-            jax.ShapeDtypeStruct((PENCILS, CHUNK, LANES), bf16),
-            jax.ShapeDtypeStruct((EDGE, WIDTH, STICKS_DEV), bf16),
-        ),
+        out_shape=(ROWS_SHAPE, BANDS_SHAPE),
         grid=(1,),
         in_specs=[
             pl.BlockSpec(memory_space=pltpu.SMEM),
-            whole(),
+            pl.BlockSpec((PENCILS, 8, LANES), lambda i: (0, CHUNK // 8, 0)),
             whole(),
             pl.BlockSpec((EDGE, WIDTH, STICKS_DEV), lambda i: (0, 0, 0)),
             whole(),
             whole(),
+            HBM,
+            HBM,
         ],
-        out_specs=(whole(), whole()),
+        out_specs=(HBM, HBM),
+        input_output_aliases={6: 0, 7: 1},
+        scratch_shapes=spread_scratch() + [VMEM((EDGE, WIDTH, STICKS_DEV), bf16), pltpu.SemaphoreType.DMA(())],
         compiler_params=params(16),
         name="edge",
-    )(keep, total, position, bands, upper, pair)
-
-
-def grid_kernel(rows_ref, potential_ref, third_ref, second_ref, back_second_ref, back_third_ref, out_ref, wide_ref, back_ref):
-    for t in range(3):
-        wide_ref[t] = rows_ref[:, :, 128 * t : 128 * t + 128].astype(f32).reshape(ROWS, 128)
-
-    def plane(x, carry):
-        rows = pl.ds(x, GBOX, stride=X_DEV)
-        section = jnp.concatenate([wide_ref[t, rows, :] for t in range(3)], axis=1).astype(bf16)
-        field = potential_ref[x]
-        results = []
-        for b in range(EDGE):
-            lanes = section[:, 128 * b : 128 * b + 256]
-            two = dot(lanes, third_ref[b]).astype(bf16)
-            stacked = jnp.concatenate([two[:, :GRID], two[:, 256 : 256 + GRID]], axis=0)
-            space = dot(second_ref[...], stacked)
-            scaled = jnp.concatenate([space[:GRID] * field, space[GRID:] * field], axis=0).astype(bf16)
-            one = dot(back_second_ref[...], scaled).astype(bf16)
-            results.append(dot(one[:GBOX], back_third_ref[b, :GRID, :]) + dot(one[GBOX:], back_third_ref[b, GRID:, :]))
-        back_ref[0, rows, :] = results[0][:, :128]
-        back_ref[1, rows, :] = results[0][:, 128:] + results[1][:, :128]
-        back_ref[2, rows, :] = results[1][:, 128:]
+    )(keep, sums, position, bands, upper, pair, rows_buffer, ortho_buffer)
+
+
+PARTS = 4
+PLANES = 2
+
+
+def grid_kernel(rows_hbm, potential_hbm, third_hbm, second_hbm, back_second_hbm, back_third_hbm, _, out_hbm, *scratch):
+    rows_ref, wide_ref, back_ref, done_ref, potential_ref, third_ref, second_ref, back_second_ref, back_third_ref = scratch[:9]
+    row_sems, plane_sems, const_sems, out_sems = scratch[9:]
+    group = PENCILS // PARTS
+    row_copies = [
+        start_copy(rows_hbm.at[group * g : group * (g + 1), :CHUNK, :], rows_ref.at[group * g : group * (g + 1)], row_sems.at[g])
+        for g in range(PARTS)
+    ]
+    consts = ((third_hbm, third_ref), (second_hbm, second_ref), (back_second_hbm, back_second_ref), (back_third_hbm, back_third_ref))
+    const_copies = [start_copy(source, target, const_sems.at[k]) for k, (source, target) in enumerate(consts)]
+    for x in range(X_DEV):
+        start_copy(potential_hbm.at[x], potential_ref.at[x], plane_sems.at[x])
+    span = group * CHUNK
+    for g in range(PARTS):
+        row_copies[g].wait()
+        block = rows_ref[group * g : group * (g + 1)]
+        for t in range(3):
+            wide_ref[t, span * g : span * (g + 1), :] = block[:, :, 128 * t : 128 * t + 128].astype(f32).reshape(span, 128)
+    for copy in const_copies:
+        copy.wait()
+
+    def planes(step, carry):
+        for u in range(PLANES):
+            x = PLANES * step + u
+            pltpu.make_async_copy(potential_hbm.at[x], potential_ref.at[x], plane_sems.at[x]).wait()
+        work = []
+        for u in range(PLANES):
+            x = PLANES * step + u
+            rows = pl.ds(x, GBOX, stride=X_DEV)
+            section = jnp.concatenate([wide_ref[t, rows, :] for t in range(3)], axis=1).astype(bf16)
+            field = potential_ref[x]
+            results = []
+            for b in range(EDGE):
+                two = dot(section[:, 128 * b : 128 * b + 256], third_ref[b]).astype(bf16)
+                stacked = jnp.concatenate([two[:, :GRID], two[:, 256 : 256 + GRID]], axis=0)
+                space = dot(second_ref[...], stacked)
+                scaled = jnp.concatenate([space[:GRID] * field, space[GRID:] * field], axis=0).astype(bf16)
+                one = dot(back_second_ref[...], scaled).astype(bf16)
+                results.append(dot(one[:GBOX], back_third_ref[b, :GRID, :]) + dot(one[GBOX:], back_third_ref[b, GRID:, :]))
+            work.append((rows, results))
+        for rows, results in work:
+            back_ref[0, rows, :] = results[0][:, :128]
+            back_ref[1, rows, :] = results[0][:, 128:] + results[1][:, :128]
+            back_ref[2, rows, :] = results[1][:, 128:]
         return carry
 
-    lax.fori_loop(0, X_DEV, plane, 0)
-    for t in range(3):
-        out_ref[:, :, 128 * t : 128 * t + 128] = back_ref[t].reshape(PENCILS, CHUNK, 128).astype(bf16)
-
-
-def on_grid(rows, potential, consts):
+    lax.fori_loop(0, X_DEV // PLANES, planes, 0)
+    out_copies = []
+    for g in range(PARTS):
+        for t in range(3):
+            part = back_ref[t, span * g : span * (g + 1), :].reshape(group, CHUNK, 128)
+            done_ref[group * g : group * (g + 1), :, 128 * t : 128 * t + 128] = part.astype(bf16)
+        out_copies.append(
+            start_copy(done_ref.at[group * g : group * (g + 1)], out_hbm.at[group * g : group * (g + 1)], out_sems.at[g])
+        )
+    for copy in out_copies:
+        copy.wait()
+
+
+def on_grid(rows, potential, consts, buffer):
+    flops = 2 * EDGE * X_DEV * (96 * 256 * 512 + 384 * 256 * 256 * 2 + 96 * 512 * 256)
     third, second, back_second, back_third = consts
-    flops = 2 * EDGE * X_DEV * (96 * 256 * 512 + 384 * 256 * 256 * 2 + 96 * 512 * 256)
+    DMA = pltpu.SemaphoreType.DMA
     return pl.pallas_call(
         grid_kernel,
-        out_shape=jax.ShapeDtypeStruct((PENCILS, CHUNK, LANES), bf16),
-        in_specs=[whole()] * 6,
-        out_specs=whole(),
-        scratch_shapes=[VMEM((3, ROWS, 128), f32), VMEM((3, ROWS, 128), f32)],
-        compiler_params=params(16),
+        out_shape=ROWS_SHAPE,
+        in_specs=[HBM] * 7,
+        out_specs=HBM,
+        input_output_aliases={6: 0},
+        scratch_shapes=[
+            VMEM((PENCILS, CHUNK, LANES), bf16),
+            VMEM((3, ROWS, 128), f32),
+            VMEM((3, ROWS, 128), f32),
+            VMEM((PENCILS, CHUNK, LANES), bf16),
+            VMEM((X_DEV, GRID, GRID), f32),
+            VMEM(third.shape, bf16),
+            VMEM(second.shape, bf16),
+            VMEM(back_second.shape, bf16),
+            VMEM(back_third.shape, bf16),
+            DMA((PARTS,)),
+            DMA((X_DEV,)),
+            DMA((4,)),
+            DMA((PARTS,)),
+        ],
+        compiler_params=params(60),
         cost_estimate=pl.CostEstimate(flops=flops, bytes_accessed=8_000_000, transcendentals=0),
         name="grid",
-    )(rows, potential, third, second, back_second, back_third)
+    )(rows, potential, *consts, buffer)
 
 
 def behind_kernel(map_ref, across_ref, rows_ref, cos_ref, sin_ref, bands_ref, out_ref):
@@ -303,27 +393,19 @@
     return lax.all_to_all(blocks, "pencil", split_axis=0, concat_axis=0, tiled=True)
 
 
-def total_over_pencil(value):
-    for bits in ((2, 4, 6), (8, 1, 9)):
-        others = [lax.ppermute(value, "pencil", [(i, i ^ bit) for i in range(PENCILS)]) for bit in bits]
-        value = (value + others[0]) + (others[1] + others[2])
-    return value
-
-
 def update(wavefunctions, potential, keep_mask, stick_map):
     first, pair, *grid_consts = [jnp.asarray(c) for c in constants()]
     bands = jnp.transpose(wavefunctions, (0, 2, 1))
     slices = lax.axis_size("cuts")
     upper = lax.ppermute(bands[EDGE:], "cuts", [(i, i + 1) for i in range(slices - 1)])
     position = stick_map.reshape(1, STICKS_DEV)
-    inner_rows = ahead(position, bands, pair)
-    inner_rows = exchange(inner_rows)
-    total = total_over_pencil(stats(upper, bands))
-    edge_rows, ortho = edge_ahead(keep_mask, total, position, bands, upper, pair)
+    inner_rows, ortho, edge_rows, inner_buffer, edge_buffer = ahead(position, bands, pair)
+    inner_rows = exchange(stats(upper, bands, inner_rows))
+    edge_rows, ortho = edge_ahead(keep_mask, inner_rows, position, bands, upper, pair, edge_rows, ortho)
     edge_rows = exchange(edge_rows)
     cos, sin = build_matrix(position, first)
-    inner_back = exchange(on_grid(inner_rows, potential, grid_consts))
-    edge_back = exchange(on_grid(edge_rows, potential, grid_consts))
+    inner_back = exchange(on_grid(inner_rows, potential, grid_consts, inner_buffer))
+    edge_back = exchange(on_grid(edge_rows, potential, grid_consts, edge_buffer))
     across = lax.axis_index("pencil").reshape(1).astype(jnp.int32)
     inner_out = behind(position, across, inner_back, cos, sin, bands, 1)
     out = behind(position, across, edge_back, cos, sin, ortho, 0, inner_out)

time: 151 us -> 151 us (level)
  blocking collectives: 0 us -> 38.4 us
  starting transfers between devices: 44.8 us -> 13 us
  local copies, waits for them, and re-layouts: 19.5 us -> 10.2 us
  Pallas kernels: 41.3 us -> 50 us
  waiting for transfers between devices: 42.9 us -> 38.4 us
    all_to_all x0 -> x1, blocking collectives: none -> 38.4 us  [exchange(): lax.all_to_all(blocks, 'pencil', split_axis=0, concat_axis=0, tiled=True)]
    all_to_all x4 -> x3, starting transfers between devices: 27.7 us -> 11.1 us  [exchange(): lax.all_to_all(blocks, 'pencil', split_axis=0, concat_axis=0, tiled=True)]
    ppermute x6 -> x0, starting transfers between devices: 15 us -> none  [total_over_pencil(): lax.ppermute(value, 'pencil', [(i, i ^ bit) for i in range(PENCILS)])]
    all_to_all x4 -> x3, waiting for transfers between devices: 24.1 us -> 35.2 us  [exchange(): lax.all_to_all(blocks, 'pencil', split_axis=0, concat_axis=0, tiled=True)]
    unnamed x50 -> x30, local copies, waits for them, and re-layouts: 18.8 us -> 7.79 us
    ppermute x6 -> x0, waiting for transfers between devices: 9.99 us -> none  [total_over_pencil(): lax.ppermute(value, 'pencil', [(i, i ^ bit) for i in range(PENCILS)])]
    pallas_call x5, Pallas kernels: 35.2 us -> 43.9 us  [the longest x2 35.2 us: on_grid(): pl.pallas_call(grid_kernel, out_shape=ROWS_SHAPE, in_specs=[HBM] * 7, out...]
    ppermute x1, waiting for transfers between devices: 8.81 us -> 3.27 us  [update(): lax.ppermute(bands[EDGE:], 'cuts', [(i, i + 1) for i in range(slices - 1)])]
  transfers between devices with their start and end apart: 11 -> 4, of which waited for: 8 -> 4; matrix products, arithmetic and copies ran while one was open for 0% -> 1% of each run, Pallas kernels for 24% -> 28%
where the time goes in v3:
time: 151 us; the launch traced here: 150 us
  Pallas kernels  50 us (33%)
  waiting for transfers between devices  38.4 us (25%)
  blocking collectives  38.4 us (25%)
  starting transfers between devices  13 us (9%)
  local copies, waits for them, and re-layouts  10.2 us (7%)
    all_to_all x1, blocking collectives, exchange(): lax.all_to_all(blocks, 'pencil', split_axis=0, concat_axis=0, tiled=True)  38.4 us
    pallas_call x2, Pallas kernels, on_grid(): pl.pallas_call(grid_kernel, out_shape=ROWS_SHAPE, in_specs=[HBM] * 7, out...  35.2 us
    all_to_all x3, waiting for transfers between devices, exchange(): lax.all_to_all(blocks, 'pencil', split_axis=0, concat_axis=0, tiled=True)  35.2 us
    all_to_all x3, starting transfers between devices, exchange(): lax.all_to_all(blocks, 'pencil', split_axis=0, concat_axis=0, tiled=True)  11.1 us
    unnamed x30, local copies, waits for them, and re-layouts  7.79 us
    pallas_call x2, Pallas kernels, behind(): pl.pallas_call(kernel, out_shape=jax.ShapeDtypeStruct((2 * EDGE, WIDTH, S...  4.93 us
    pallas_call x1, Pallas kernels, edge_ahead(): pl.pallas_call(edge_kernel, out_shape=(ROWS_SHAPE, BANDS_SHAPE), grid=(1,...  4.34 us
    pallas_call x1, Pallas kernels, ahead(): pl.pallas_call(ahead_kernel, out_shape=(jax.ShapeDtypeStruct((PENCILS, CH...  3.7 us
  transfers between devices with their start and end apart: 4, of which 4 were waited for; matrix products, arithmetic and copies ran while one was open for 1% of the time, Pallas kernels for 28%

profile of v3, /device:TPU:10, one launch (start us, length us, event | category | flops | bytes accessed | tf_op | source)
XLA Modules:
  0.0 150.2 jit_solution(13409754747339727537)
XLA Ops:
  0.0 1.2 slice.4
  1.2 1.9 %collective-permute-start = (bf16[2,192,576]{2,1,0:T(8,128)(2,1)S(1)}, bf16[2,192,576]{2,1,0:T(8,128)(2,1)S(1)}, u32[]{:S(2)}, u32[]{:S(2)}) collective-permute-start(bf16[2,192,576]{2,1,0:T(8,128)(2,1)S(1)} %slice.4), channel_id=1, source_target_pairs={{0,16},{16,32},{32,48},{48,64},{64,80},{80,96},{96,112},{112,128},... | collective-permute-start | bytes 1327112 | tf_op jit(solution)/shard_map/ppermute | solution.py:400
  3.1 1.2 reshape.6.map_ref.refs_0_
  4.3 3.7 %ahead.1 = (bf16[16,80,384]{2,1,0:T(8,128)(2,1)}, bf16[2,192,576]{2,1,0:T(8,128)(2,1)}, bf16[16,72,384]{2,1,0:T(8,128)(2,1)}, bf16[16,72,384]{2,1,0:T(8,128)(2,1)}, bf16[16,72,384]{2,1,0:T(8,128)(2,1)}) custom-call(s32[1,576]{1,0:T(1,128)} %reshape.6.map_ref.refs_0_, bf16[4,192,576]{2,1,0:T(8,128)(2,1)} %bitcast.4, bf16[384,384]{1,0:T(8,128)(2,1)} %constant.17.clone.pair_ref), custom_call_target="tpu_custom_call" | custom-call | tf_op jit(solution)/shard_map/ahead/pallas_call | solution.py:194
  8.0 3.3 %collective-permute-done.upper_ref = bf16[2,192,576]{2,1,0:T(8,128)(2,1)S(1)} collective-permute-done((bf16[2,192,576]{2,1,0:T(8,128)(2,1)S(1)}, bf16[2,192,576]{2,1,0:T(8,128)(2,1)S(1)}, u32[]{:S(2)}, u32[]{:S(2)}) %collective-permute-start) | collective-permute-done | bytes 442400 | tf_op jit(solution)/shard_map/ppermute | solution.py:400
  11.3 1.2 copy-done.4
  12.5 0.6 stats.1
  13.2 0.0 copy-start.10
  13.2 0.0 copy-start.13
  13.2 38.4 %all_to_all.20.sums_ref.rows_hbm = bf16[16,80,384]{2,1,0:T(8,128)(2,1)S(1)} all-to-all(bf16[16,80,384]{2,1,0:T(8,128)(2,1)S(1)} %stats.1), channel_id=1, replica_groups=mesh['cuts'=16,'pencil'=16] {'pencil'}, dimensions={0} | all-to-all | bytes 1966080 | tf_op jit(solution)/shard_map/all_to_all | solution.py:393
  51.6 0.0 copy-done.7
  51.6 4.3 %edge.1 = (bf16[16,72,384]{2,1,0:T(8,128)(2,1)}, bf16[2,192,576]{2,1,0:T(8,128)(2,1)S(1)}) custom-call(s32[1,2,2]{2,1,0:T(2,128)S(1)} %copy-done.13, bf16[16,80,384]{2,1,0:T(8,128)(2,1)S(1)} %all_to_all.20.sums_ref.rows_hbm, s32[1,576]{1,0:T(1,128)S(1)} %copy-done.12, ...), custom_call_target="tpu_custom_call", output_to_operand_aliasing={{0}: (6, {}), {1}: (7, {})} | custom-call | tf_op jit(solution)/shard_map/edge/pallas_call | solution.py:231
  56.0 0.8 copy-done.8
  56.8 3.6 %all-to-all-start.1 = ((bf16[16,72,384]{2,1,0:T(8,128)(2,1)}), bf16[16,72,384]{2,1,0:T(8,128)(2,1)S(1)}, u32[]{:S(2)}, u32[]{:S(2)}) async-start(bf16[16,72,384]{2,1,0:T(8,128)(2,1)} %get-tuple-element.17), calls=%async_computation.1 | async-start | bytes 1769472 | tf_op jit(solution)/shard_map/all_to_all | solution.py:393
  60.4 17.6 %grid.3 = bf16[16,72,384]{2,1,0:T(8,128)(2,1)} custom-call(bf16[16,80,384]{2,1,0:T(8,128)(2,1)} %copy-done.3, f32[12,192,192]{2,1,0:T(8,128)} %potential_hbm.3, bf16[2,256,512]{2,1,0:T(8,128)(2,1)} %constant.18.clone.third_hbm, bf16[384,192]{1,0:T(8,128)(2,1)} %constant.19.clone.second_hbm, ...), custom_call_target="tpu_custom_call", output_to_operand_aliasing={{}: (6, {})} | custom-call | flops 3623878656 | bytes 8000000 | tf_op jit(solution)/shard_map/grid/pallas_call | solution.py:320
  78.0 7.6 %all-to-all-done.1.rows_hbm = bf16[16,72,384]{2,1,0:T(8,128)(2,1)S(1)} async-done(((bf16[16,72,384]{2,1,0:T(8,128)(2,1)}), bf16[16,72,384]{2,1,0:T(8,128)(2,1)S(1)}, u32[]{:S(2)}, u32[]{:S(2)}) %all-to-all-start.1) | async-done | bytes 884768 | tf_op jit(solution)/shard_map/all_to_all | solution.py:393
  85.7 3.6 %all-to-all-start.3 = ((bf16[16,72,384]{2,1,0:T(8,128)(2,1)}), bf16[16,72,384]{2,1,0:T(8,128)(2,1)S(1)}, u32[]{:S(2)}, u32[]{:S(2)}) async-start(bf16[16,72,384]{2,1,0:T(8,128)(2,1)} %grid.3), calls=%async_computation.3 | async-start | bytes 1769472 | tf_op jit(solution)/shard_map/all_to_all | solution.py:393
  89.3 0.0 copy-done.14
  89.3 17.6 %grid.2 = bf16[16,72,384]{2,1,0:T(8,128)(2,1)} custom-call(bf16[16,72,384]{2,1,0:T(8,128)(2,1)} %copy-done.14, f32[12,192,192]{2,1,0:T(8,128)} %potential_hbm.3, bf16[2,256,512]{2,1,0:T(8,128)(2,1)} %constant.18.clone.third_hbm, bf16[384,192]{1,0:T(8,128)(2,1)} %constant.19.clone.second_hbm, ...), custom_call_target="tpu_custom_call", output_to_operand_aliasing={{}: (6, {})} | custom-call | flops 3623878656 | bytes 8000000 | tf_op jit(solution)/shard_map/grid/pallas_call | solution.py:320
  106.9 8.8 %all-to-all-done.3.rows_ref = bf16[16,72,384]{2,1,0:T(8,128)(2,1)S(1)} async-done(((bf16[16,72,384]{2,1,0:T(8,128)(2,1)}), bf16[16,72,384]{2,1,0:T(8,128)(2,1)S(1)}, u32[]{:S(2)}, u32[]{:S(2)}) %all-to-all-start.3) | async-done | bytes 884768 | tf_op jit(solution)/shard_map/all_to_all | solution.py:393
  115.7 3.8 %all-to-all-start.2 = ((bf16[16,72,384]{2,1,0:T(8,128)(2,1)}), bf16[16,72,384]{2,1,0:T(8,128)(2,1)S(1)}, u32[]{:S(2)}, u32[]{:S(2)}) async-start(bf16[16,72,384]{2,1,0:T(8,128)(2,1)} %grid.2), calls=%async_computation.2 | async-start | bytes 1769472 | tf_op jit(solution)/shard_map/all_to_all | solution.py:393
  119.5 0.0 copy-start.11
  119.5 1.1 copy-done.11
  120.6 1.2 matrix.1
  121.8 0.0 copy-start.6
  121.8 1.2 copy-done.6
  123.0 2.5 %behind.2.refs_6_ = bf16[4,192,576]{2,1,0:T(8,128)(2,1)} custom-call(s32[1,576]{1,0:T(1,128)S(1)} %copy-done.12, s32[1]{0:T(128)} %bitcast.across_ref.refs_1_, bf16[16,72,384]{2,1,0:T(8,128)(2,1)S(1)} %copy-done.6, bf16[1152,576]{1,0:T(8,128)(2,1)S(1)} %get-tuple-element.19.cos_ref.refs_3_, bf16[1152,576]{1,0:T(8,128)(2,1)S(1)} %get-tuple-element.20.sin_ref.refs_4_, ...), custom_call_target="tpu_custom_call" | custom-call | tf_op jit(solution)/shard_map/behind/pallas_call | solution.py:380
  125.4 1.1 copy-done.1
  126.6 18.8 %all-to-all-done.2.refs_2_ = bf16[16,72,384]{2,1,0:T(8,128)(2,1)S(1)} async-done(((bf16[16,72,384]{2,1,0:T(8,128)(2,1)}), bf16[16,72,384]{2,1,0:T(8,128)(2,1)S(1)}, u32[]{:S(2)}, u32[]{:S(2)}) %all-to-all-start.2) | async-done | bytes 884768 | tf_op jit(solution)/shard_map/all_to_all | solution.py:393
  145.3 1.4 copy-done.2
  146.7 1.0 copy-done.9
  147.8 2.5 %behind.3 = bf16[4,192,576]{2,1,0:T(8,128)(2,1)} custom-call(s32[1,576]{1,0:T(1,128)S(1)} %copy-done.12, s32[1]{0:T(128)} %bitcast.across_ref.refs_1_, bf16[16,72,384]{2,1,0:T(8,128)(2,1)S(1)} %all-to-all-done.2.refs_2_, bf16[1152,576]{1,0:T(8,128)(2,1)S(1)} %get-tuple-element.19.cos_ref.refs_3_, ...), custom_call_target="tpu_custom_call", output_to_operand_aliasing={{}: (6, {})} | custom-call | tf_op jit(solution)/shard_map/behind/pallas_call | solution.py:380
  (17 shorter events, 0.0 us)
Async XLA Ops:
  0.0 11.3 %copy-start = (bf16[4,576,192]{1,2,0:T(8,128)(2,1)S(1)}, bf16[4,576,192]{1,2,0:T(8,128)(2,1)}, u32[]{:S(2)}) copy-start(bf16[4,576,192]{1,2,0:T(8,128)(2,1)} %param.10) | copy-start | bytes 2654212
  1.2 10.1 %collective-permute-start = (bf16[2,192,576]{2,1,0:T(8,128)(2,1)S(1)}, bf16[2,192,576]{2,1,0:T(8,128)(2,1)S(1)}, u32[]{:S(2)}, u32[]{:S(2)}) collective-permute-start(bf16[2,192,576]{2,1,0:T(8,128)(2,1)S(1)} %slice.4), channel_id=1, source_target_pairs={{0,16},{16,32},{32,48},{48,64},{64,80},{80,96},{96,112},{112,128},... | collective-permute-start | bytes 1327112 | tf_op jit(solution)/shard_map/ppermute | solution.py:400
  11.3 1.2 copy-start.4
  13.2 38.4 %copy-start.7 = (bf16[2,192,576]{2,1,0:T(8,128)(2,1)S(1)}, bf16[2,192,576]{2,1,0:T(8,128)(2,1)}, u32[]{:S(2)}) copy-start(bf16[2,192,576]{2,1,0:T(8,128)(2,1)} %get-tuple-element.16.__) | copy-start | bytes 1327108
  13.2 38.4 %copy-start.10 = (bf16[384,384]{1,0:T(8,128)(2,1)S(1)}, bf16[384,384]{1,0:T(8,128)(2,1)}, u32[]{:S(2)}) copy-start(bf16[384,384]{1,0:T(8,128)(2,1)} %constant.17.clone.pair_ref) | copy-start | bytes 884740
  13.2 38.4 %copy-start.12 = (s32[1,576]{1,0:T(1,128)S(1)}, s32[1,576]{1,0:T(1,128)}, u32[]{:S(2)}) copy-start(s32[1,576]{1,0:T(1,128)} %reshape.6.map_ref.refs_0_) | copy-start | bytes 6916
  13.2 38.4 %copy-start.13 = (s32[1,2,2]{2,1,0:T(2,128)S(1)}, s32[1,2,2]{2,1,0:T(2,128)}, u32[]{:S(2)}) copy-start(s32[1,2,2]{2,1,0:T(2,128)} %keep_ref.1) | copy-start | bytes 52
  51.6 4.4 %copy-start.3 = (bf16[16,80,384]{2,1,0:T(8,128)(2,1)}, bf16[16,80,384]{2,1,0:T(8,128)(2,1)S(1)}, u32[]{:S(2)}) copy-start(bf16[16,80,384]{2,1,0:T(8,128)(2,1)S(1)} %all_to_all.20.sums_ref.rows_hbm) | copy-start | bytes 2949124
  56.0 0.8 copy-start.8
  56.8 28.9 %all-to-all-start.1 = ((bf16[16,72,384]{2,1,0:T(8,128)(2,1)}), bf16[16,72,384]{2,1,0:T(8,128)(2,1)S(1)}, u32[]{:S(2)}, u32[]{:S(2)}) async-start(bf16[16,72,384]{2,1,0:T(8,128)(2,1)} %get-tuple-element.17), calls=%async_computation.1 | async-start | bytes 1769472 | tf_op jit(solution)/shard_map/all_to_all | solution.py:393
  85.7 3.6 %copy-start.14 = (bf16[16,72,384]{2,1,0:T(8,128)(2,1)}, bf16[16,72,384]{2,1,0:T(8,128)(2,1)S(1)}, u32[]{:S(2)}) copy-start(bf16[16,72,384]{2,1,0:T(8,128)(2,1)S(1)} %all-to-all-done.1.rows_hbm) | copy-start | bytes 2654212
  85.7 30.0 %all-to-all-start.3 = ((bf16[16,72,384]{2,1,0:T(8,128)(2,1)}), bf16[16,72,384]{2,1,0:T(8,128)(2,1)S(1)}, u32[]{:S(2)}, u32[]{:S(2)}) async-start(bf16[16,72,384]{2,1,0:T(8,128)(2,1)} %grid.3), calls=%async_computation.3 | async-start | bytes 1769472 | tf_op jit(solution)/shard_map/all_to_all | solution.py:393
  115.7 3.8 %copy-start.5 = (bf16[16,72,384]{2,1,0:T(8,128)(2,1)}, bf16[16,72,384]{2,1,0:T(8,128)(2,1)S(1)}, u32[]{:S(2)}) copy-start(bf16[16,72,384]{2,1,0:T(8,128)(2,1)S(1)} %all-to-all-done.3.rows_ref) | copy-start | bytes 2654212
  115.7 29.7 %all-to-all-start.2 = ((bf16[16,72,384]{2,1,0:T(8,128)(2,1)}), bf16[16,72,384]{2,1,0:T(8,128)(2,1)S(1)}, u32[]{:S(2)}, u32[]{:S(2)}) async-start(bf16[16,72,384]{2,1,0:T(8,128)(2,1)} %grid.2), calls=%async_computation.2 | async-start | bytes 1769472 | tf_op jit(solution)/shard_map/all_to_all | solution.py:393
  119.5 1.1 copy-start.11
  121.8 1.2 copy-start.6
  125.4 1.1 copy-start.1
  145.3 1.4 copy-start.2
  146.7 1.0 copy-start.9
